TPU v7x, 256 devices: a whole 4x4x8 slice. The times are simulated.
256 devices in a mesh: coh: 4 (over y), lat: 4 (over x), lon: 16 (over z, core).
Axes of the slice: x: 4, y: 4, z: 8, core: 2. Of those that a mesh axis runs over, the one named last changes fastest.
Arguments:
- saved_period_abundance: bfloat16 [2, 128, 256, 4096], P(None, 'coh', 'lat', 'lon'), may hold values from 0.099609375 to 2
- final_abundance_sensitivity: bfloat16 [128, 256, 4096], P('coh', 'lat', 'lon'), may hold values from -6 to 6
- prey_biomass: float32 [2, 256, 4096], P(None, 'lat', 'lon'), may hold values from 0.2 to 2
- water_heat_field: float32 [2, 256, 4096], P(None, 'lat', 'lon'), may hold values from 10 to 30
- marine_indicator: int32 [256, 4096], P('lat', 'lon'), may hold values 0 or 1
- fishing_pressure: float32 [256, 4096], P('lat', 'lon'), may hold values from 0.1 to 2
- offspring_yield: float32 [256, 4096], P('lat', 'lon'), may hold values from 2 to 20
- death_fraction: float32 [128], P('coh'), may hold values from 0.01 to 0.5
- gear_vulnerability: float32 [128], P('coh'), may hold values from 0.05 to 0.5
- spreading_coefficient: float32 [128], P('coh'), may hold values from 0.02 to 0.12
- directed_drift_rate: float32 [128], P('coh'), may hold values from 0.01 to 0.06
- favoured_thermal_level: float32 [128], P('coh'), may hold values from 12 to 28
- breeding_contribution: float32 [128], P('coh'), may hold values from 0.005 to 0.03
- landing_error_sensitivity: float32 [2048, 2, 128], P(('lat', 'lon'), None, 'coh'), may hold values from -6 to 6
- fleet_east_piece: int32 [2048, 1], P(('lat', 'lon')), may hold values from 0 to 15; in each aligned block of 32 rows (0 to 31, 32 to 63, ...) at most 3 rows name the same one
- fleet_north_piece: int32 [2048], P(('lat', 'lon')), may hold values from 0 to 3
- fleet_area_patch: int32 [2048], P(('lat', 'lon')), may hold values from 0 to 31
- fleet_age_bounds: int32 [2048, 2], P(('lat', 'lon')), may hold values from 0 to 128, as said below
Outputs:
- density_grad: float32 [128, 256, 4096], P('coh', 'lat', 'lon')
- recruit_grad: float32 [256, 4096], P('lat', 'lon')
Inputs may be any that keep to these rules, and one draw needn't show every extreme that they name: `fleet_east_piece`: among the rows of one device, at most 3 name the same longitude tile, and some longitude tile is named by exactly 3 of them. `fleet_age_bounds`: in every row the first entry is below the second.
All inputs are finite; a program needn't handle non-finite values. No bound on the sum of `marine_indicator` on one device may be relied on, other than what follows from the above.
Results may differ from a plain program's by a relative error of at most 0.0003.
Values sent between devices are 32-bit elements; how exact they have to be, the bound alone decides.
A program may use at most 64 MiB of HBM per device.

v0:
```python
import jax
import jax.numpy as jnp
from jax import lax
from jax.sharding import PartitionSpec as P

BY = 16
BX = 32


thermal_tolerance_spread = 4.0
highest = lax.Precision.HIGHEST


def from_root(value, axis, source):
    kept = jnp.where(lax.axis_index(axis) == source, value, 0).astype(value.dtype)
    return lax.psum(kept, axis)


def shifted(block, axis, distance):
    devices = range(lax.axis_size(axis))
    route = [(i - distance, i) for i in devices if i - distance in devices]
    return lax.ppermute(block, axis, route)


def with_halo(x, sides, width):
    for axis, dim in sides:
        devices, length = (lax.axis_size(axis), x.shape[dim])
        up = [(i, (i + 1) % devices) for i in range(devices - 1)]
        down = [(j, i) for i, j in up]
        last = lax.slice_in_dim(x, length - width, length, axis=dim)
        first = lax.slice_in_dim(x, 0, width, axis=dim)
        before = lax.ppermute(last, axis, up)
        after = lax.ppermute(first, axis, down)
        x = jnp.concatenate([before, x, after], axis=dim)
    return x


def views(rimmed):
    return (
        rimmed[..., :-2, 1:-1],
        rimmed[..., 2:, 1:-1],
        rimmed[..., 1:-1, 2:],
        rimmed[..., 1:-1, :-2],
    )


def fold_rows(base, nblocks, pieces):
    values, targets = pieces
    wanted = (base + jnp.arange(nblocks)).astype(jnp.float32)
    onehot = (targets[None, :] == wanted[:, None]).astype(jnp.float32)
    return jnp.dot(onehot, values, precision=highest)


def shards(
    saved_period_abundance,
    final_abundance_sensitivity,
    prey_biomass,
    water_heat_field,
    marine_indicator,
    fishing_pressure,
    offspring_yield,
    death_fraction,
    gear_vulnerability,
    spreading_coefficient,
    directed_drift_rate,
    favoured_thermal_level,
    breeding_contribution,
    landing_error_sensitivity,
    fleet_east_piece,
    fleet_north_piece,
    fleet_area_patch,
    fleet_age_bounds,
):
    months, ages_here, rows_y, rows_x = saved_period_abundance.shape
    coh_pos = lax.axis_index("coh")
    lat_pos = lax.axis_index("lat")
    lon_pos = lax.axis_index("lon")
    lon_count = lax.axis_size("lon")
    total_ages = ages_here * lax.axis_size("coh")
    cohort_age = coh_pos * ages_here + jnp.arange(ages_here)
    maturity = (cohort_age + 1).astype(jnp.float32) / total_ages * breeding_contribution
    sea_field = marine_indicator.astype(jnp.float32)
    row_count = landing_error_sensitivity.shape[0]
    blocks_y = rows_y // BY
    blocks_x = rows_x // BX
    nblocks = blocks_y * blocks_x
    inside = (cohort_age[None, :] >= fleet_age_bounds[:, 0:1]) & (
        cohort_age[None, :] < fleet_age_bounds[:, 1:2]
    )
    masked = (landing_error_sensitivity * inside[:, None, :].astype(jnp.float32)).reshape(
        row_count, months * ages_here
    )
    place_id = (
        (fleet_north_piece * lon_count + fleet_east_piece[:, 0]) * nblocks + fleet_area_patch
    ).astype(jnp.float32)
    block_values = fold_rows(
        (lat_pos * lon_count + lon_pos) * nblocks,
        nblocks,
        (
            lax.all_gather(masked, ("lat", "lon"), axis=0, tiled=True),
            lax.all_gather(place_id, ("lat", "lon"), axis=0, tiled=True),
        ),
    )
    partial_spawn = jnp.stack(
        [
            jnp.tensordot(
                maturity,
                saved_period_abundance[period_counter].astype(jnp.float32),
                axes=1,
                precision=highest,
            )
            for period_counter in range(months)
        ]
    )
    survive = jnp.exp(
        -death_fraction[:, None, None] - gear_vulnerability[:, None, None] * fishing_pressure[None]
    )
    adjoint = final_abundance_sensitivity.astype(jnp.float32)
    grad_recruit = jnp.zeros((rows_y, rows_x), jnp.float32)
    spawn_total = lax.psum(partial_spawn, "coh")
    for period_counter in range(months - 1, -1, -1):
        spawning = spawn_total[period_counter]
        first_plane = from_root(adjoint[0], "coh", 0)
        next_plane = shifted(adjoint[0], "coh", -1)
        extended = jnp.concatenate(
            [
                adjoint[1:],
                next_plane[None],
                prey_biomass[period_counter][None],
                water_heat_field[period_counter][None],
                sea_field[None],
            ],
            axis=0,
        )
        rimmed = with_halo(extended, (("lat", 1), ("lon", 2)), 1)
        later_rim = rimmed[:ages_here]
        forage_rim = rimmed[ages_here]
        thermal_halo_border = rimmed[ages_here + 1]
        sea_rim = rimmed[ages_here + 2]
        thermal_departure = (
            thermal_halo_border[None] - favoured_thermal_level[:, None, None]
        ) / thermal_tolerance_spread
        habitat = sea_rim * forage_rim / (1.0 + thermal_departure * thermal_departure)
        later = later_rim[:, 1:-1, 1:-1]
        habitat_here = habitat[:, 1:-1, 1:-1]
        outflow = jnp.zeros_like(later)
        for sea_next, hab_next, adj_next in zip(views(sea_rim), views(habitat), views(later_rim)):
            flow_rate = (
                sea_field
                * sea_next
                * (
                    spreading_coefficient[:, None, None]
                    + jnp.maximum(
                        directed_drift_rate[:, None, None] * (hab_next - habitat_here), 0.0
                    )
                )
            )
            outflow = outflow + flow_rate * (later - adj_next)
        after_move = later - outflow
        ratio = 1.0 / (1.0 + spawning)
        recruit_term = first_plane * sea_field * offspring_yield * ratio * ratio
        month_values = block_values[
            :, period_counter * ages_here : (period_counter + 1) * ages_here
        ]
        block_grid = month_values.reshape(blocks_y, blocks_x, ages_here).transpose(2, 0, 1)
        spread = jnp.broadcast_to(
            block_grid[:, :, None, :, None], (ages_here, blocks_y, BY, blocks_x, BX)
        )
        adjoint = (
            survive * after_move
            + recruit_term[None] * maturity[:, None, None]
            + gear_vulnerability[:, None, None]
            * fishing_pressure[None]
            * spread.reshape(ages_here, rows_y, rows_x)
        )
        grad_recruit = grad_recruit + first_plane * sea_field * spawning * ratio
    return (adjoint, grad_recruit)


def solution(mesh):
    in_specs = (
        P(None, "coh", "lat", "lon"),
        P("coh", "lat", "lon"),
        P(None, "lat", "lon"),
        P(None, "lat", "lon"),
        P("lat", "lon"),
        P("lat", "lon"),
        P("lat", "lon"),
        P("coh"),
        P("coh"),
        P("coh"),
        P("coh"),
        P("coh"),
        P("coh"),
        P(("lat", "lon"), None, "coh"),
        P(("lat", "lon"), None),
        P(("lat", "lon")),
        P(("lat", "lon")),
        P(("lat", "lon"), None),
    )
    out_specs = (P("coh", "lat", "lon"), P("lat", "lon"))
    return jax.shard_map(shards, mesh=mesh, in_specs=in_specs, out_specs=out_specs, check_vma=False)
```

profile of v0, /device:TPU:1, one launch (start us, length us, event | category | flops | bytes accessed | tf_op | source)
XLA Modules:
  0.0 356.1 jit_solution(8194302968326700372)
XLA Ops:
  7.2 1.5 convert_element_type.33
  8.7 1.3 collective-permute-start
  10.7 1.7 slice_bitcast_fusion.1
  12.4 1.0 fusion.63
  13.4 1.0 fusion.65
  15.1 1.8 constant_dynamic-update-slice_fusion.1
  17.1 54.8 %all_gather.7 = f32[2048,64]{1,0:T(8,128)S(1)} all-gather(f32[32,64]{1,0:T(8,128)S(1)} %reshape.100), channel_id=1, replica_groups=mesh['coh'=4,'lat'=4,'lon'=16] {'lat','lon'}, dimensions={0}, use_global_device_ids=true | all-gather | bytes 532480 | tf_op jit(solution)/shard_map/all_gather | solution.py:100
  72.0 1.3 dynamic-slice
  73.9 0.8 convert_dynamic-update-slice_fusion
  74.7 125.6 %all-reduce = f32[2048]{0:T(1024)S(1)} all-reduce(f32[2048]{0:T(1024)S(1)} %convert_dynamic-update-slice_fusion), channel_id=1, replica_groups=mesh['coh'=4,'lat'=4,'lon'=16] {'lat','lon'}, use_global_device_ids=true, to_apply=%add | all-reduce | flops 2048 | bytes 16384
  200.3 0.9 slice_dynamic-update-slice_fusion.3
  201.2 0.8 slice_dynamic-update-slice_fusion.2
  202.1 1.3 collective-permute-start.2
  203.4 4.0 %collective-permute-start.1 = (f32[35,1,256]{2,1,0:T(1,128)S(1)}, f32[35,1,256]{2,1,0:T(1,128)S(1)}, u32[]{:S(2)}, u32[]{:S(2)}) collective-permute-start(f32[35,1,256]{2,1,0:T(1,128)S(1)} %get-tuple-element.16), channel_id=1, source_target_pairs={{0,16},{16,32},{32,48},{1,17},{17,33},{33,49},{2,18},{18,34},{34,5... | collective-permute-start | bytes 107528 | tf_op jit(solution)/shard_map/ppermute | solution.py:32
  208.8 1.9 fusion.82
  210.7 1.9 copy.35
  212.6 2.4 collective-permute-start.3
  214.9 1.8 copy.36
  216.7 5.5 %collective-permute-start.4 = (f32[35,66,1]{1,2,0:T(1,128)S(1)}, f32[35,66,1]{1,2,0:T(1,128)S(1)}, u32[]{:S(2)}, u32[]{:S(2)}) collective-permute-start(f32[35,66,1]{1,2,0:T(1,128)S(1)} %copy.36), channel_id=1, source_target_pairs={{1,0},{2,1},{3,2},{4,3},{5,4},{6,5},{7,6},{8,7},{9,8},{10,9},{11,1... | collective-permute-start | bytes 27728 | tf_op jit(solution)/shard_map/ppermute | solution.py:33
  222.3 1.6 slice.258
  224.0 3.9 %broadcast_in_dim.18 = f32[32,4,16,8,32]{4,3,2,1,0:T(8,128)} broadcast(f32[32,4,8]{2,1,0:T(4,128)S(1)} %copy.41), dimensions={0,1,3} | broadcast | bytes 2101248 | tf_op jit(solution)/shard_map/broadcast_in_dim | solution.py:166
  227.9 7.0 %reshape.102 = f32[32,64,256]{2,1,0:T(8,128)} reshape(f32[32,4,16,8,32]{4,3,2,1,0:T(8,128)} %broadcast_in_dim.18) | data formatting | bytes 4194304 | tf_op jit(solution)/shard_map/reshape | solution.py:174
  235.5 1.6 copy.37
  237.1 1.6 copy.38
  238.7 1.0 fusion.73
  240.4 0.8 fusion.75
  242.0 1.2 slice_multiply_fusion.7
  243.2 13.6 %fusion.4 = f32[32,64,256]{2,1,0:T(8,128)S(1)} fusion(f32[32,64,256]{2,1,0:T(8,128)} %reshape.102, f32[35,66,1]{2,1,0:T(8,128)} %copy.37, f32[35,1,256]{2,1,0:T(1,128)} %copy-done.12, f32[35,64,256]{2,1,0:T(8,128)} %copy-done, f32[35,1,256]{2,1,0:T(1,128)} %copy-done.14, f32[32,66,258]{2,1,0:T(8,128)S(1)} %add_divide_fusion.1, f32[35,66,1]{2,1,0:T(8,128)} %copy.38, ...), kind=kLoop, calls=%fused_computation.11 | loop fusion | flops 25165824 | bytes 19554992 | tf_op jit(solution)/shard_map/add | solution.py:170
  256.9 1.4 collective-permute-start.5
  258.3 1.8 fusion.85
  260.1 3.1 collective-permute-done.5
  263.3 1.3 collective-permute-start.7
  264.6 4.6 %collective-permute-start.6 = (f32[35,1,256]{2,1,0:T(1,128)S(1)}, f32[35,1,256]{2,1,0:T(1,128)S(1)}, u32[]{:S(2)}, u32[]{:S(2)}) collective-permute-start(f32[35,1,256]{2,1,0:T(1,128)S(1)} %get-tuple-element.14), channel_id=1, source_target_pairs={{0,16},{16,32},{32,48},{1,17},{17,33},{33,49},{2,18},{18,34},{34,5... | collective-permute-start | bytes 107528 | tf_op jit(solution)/shard_map/ppermute | solution.py:32
  269.3 3.9 %broadcast_in_dim.20 = f32[32,4,16,8,32]{4,3,2,1,0:T(8,128)} broadcast(f32[32,4,8]{2,1,0:T(4,128)S(1)} %copy.48), dimensions={0,1,3} | broadcast | bytes 2101248 | tf_op jit(solution)/shard_map/broadcast_in_dim | solution.py:166
  273.2 7.0 %reshape.104 = f32[32,64,256]{2,1,0:T(8,128)} reshape(f32[32,4,16,8,32]{4,3,2,1,0:T(8,128)} %broadcast_in_dim.20) | data formatting | bytes 4194304 | tf_op jit(solution)/shard_map/reshape | solution.py:174
  280.6 1.9 fusion.81
  282.5 1.8 copy.42
  284.3 1.9 collective-permute-start.8
  286.2 1.8 copy.43
  288.0 2.6 collective-permute-start.9
  290.6 1.5 broadcast_select_fusion
  292.1 1.6 copy.44
  293.7 1.6 copy.45
  295.3 1.0 fusion.71
  297.1 0.8 fusion.76
  298.6 34.3 %all-reduce.5.cloned.1.call-done = f32[64,256]{1,0:T(8,128)} async-done(((f32[64,256]{1,0:T(8,128)}), f32[64,256]{1,0:T(8,128)}) %all-reduce.5.cloned.1.call-update) | async-done | bytes 65552 | tf_op jit(solution)/shard_map/psum | solution.py:16
  332.9 1.9 multiply_add_fusion
  334.9 14.3 %fusion.6 = f32[32,64,256]{2,1,0:T(8,128)} fusion(f32[32,64,256]{2,1,0:T(8,128)} %reshape.104, f32[35,66,1]{2,1,0:T(8,128)} %copy.44, f32[35,1,256]{2,1,0:T(1,128)} %copy-done.11, f32[35,64,256]{2,1,0:T(8,128)} %copy-done.1, f32[35,1,256]{2,1,0:T(1,128)} %copy-done.13, f32[32,66,258]{2,1,0:T(8,128)S(1)} %add_divide_fusion, f32[35,66,1]{2,1,0:T(8,128)} %copy.45, ...), kind=kLoop, calls=%fused_computation.13 | loop fusion | flops 25165824 | bytes 19554992 | tf_op jit(solution)/shard_map/add | solution.py:170
  (105 shorter events, 7.2 us)
Async XLA Ops:
  7.2 234.8 %all-reduce.7.cloned.1.call-start = ((), (), s32[]{:S(2)}) async-start(), calls=%async_computation.1 | async-start | bytes 393216 | tf_op jit(solution)/shard_map/psum | solution.py:16
  8.7 3.7 %copy-start.8 = (f32[32,64,256]{2,1,0:T(8,128)}, f32[32,64,256]{2,1,0:T(8,128)S(1)}, u32[]{:S(2)}) copy-start(f32[32,64,256]{2,1,0:T(8,128)S(1)} %convert_element_type.33) | copy-start | bytes 6291460
  8.7 191.6 %collective-permute-start = (f32[64,256]{1,0:T(8,128)S(1)}, f32[64,256]{1,0:T(8,128)S(1)}, u32[]{:S(2)}, u32[]{:S(2)}) collective-permute-start(f32[64,256]{1,0:T(8,128)S(1)} %slice_bitcast_fusion.5), channel_id=1, source_target_pairs={{64,0},{128,64},{192,128},{65,1},{129,65},{193,129},{66,2},{130,66... | collective-permute-start | bytes 196616 | tf_op jit(solution)/shard_map/ppermute | solution.py:22
  10.7 1.7 copy-start.28
  12.4 4.5 %copy-start.20 = (f32[32]{0:T(128)}, f32[32]{0:T(128)S(1)}, u32[]{:S(2)}) copy-start(f32[32]{0:T(128)S(1)} %multiply_multiply_fusion.4) | copy-start | bytes 388
  15.0 1.9 copy-start.27
  15.0 2.0 copy-start.19
  15.0 317.9 %all-reduce.5.cloned.1.call-start = ((), (), s32[]{:S(2)}) async-start(), calls=%async_computation | async-start | bytes 131072 | tf_op jit(solution)/shard_map/psum | solution.py:16
  15.1 186.9 %copy-start.9 = (s32[64,256]{1,0:T(8,128)S(1)}, s32[64,256]{1,0:T(8,128)}, u32[]{:S(2)}) copy-start(s32[64,256]{1,0:T(8,128)} %param.22) | copy-start | bytes 196612
  200.3 3.1 copy-start.15
  202.0 37.7 %copy-start = (f32[35,64,256]{2,1,0:T(8,128)}, f32[35,64,256]{2,1,0:T(8,128)S(1)}, u32[]{:S(2)}) copy-start(f32[35,64,256]{2,1,0:T(8,128)S(1)} %bitcast_dynamic-update-slice_fusion.1) | copy-start | bytes 6881284
  202.1 5.8 %collective-permute-start.2 = (f32[35,1,256]{2,1,0:T(1,128)S(1)}, f32[35,1,256]{2,1,0:T(1,128)S(1)}, u32[]{:S(2)}, u32[]{:S(2)}) collective-permute-start(f32[35,1,256]{2,1,0:T(1,128)S(1)} %get-tuple-element.17), channel_id=1, source_target_pairs={{16,0},{32,16},{48,32},{17,1},{33,17},{49,33},{18,2},{34,18},{50,3... | collective-permute-start | bytes 107528 | tf_op jit(solution)/shard_map/ppermute | solution.py:33
  203.4 5.0 %collective-permute-start.1 = (f32[35,1,256]{2,1,0:T(1,128)S(1)}, f32[35,1,256]{2,1,0:T(1,128)S(1)}, u32[]{:S(2)}, u32[]{:S(2)}) collective-permute-start(f32[35,1,256]{2,1,0:T(1,128)S(1)} %get-tuple-element.16), channel_id=1, source_target_pairs={{0,16},{16,32},{32,48},{1,17},{17,33},{33,49},{2,18},{18,34},{34,5... | collective-permute-start | bytes 107528 | tf_op jit(solution)/shard_map/ppermute | solution.py:32
  207.9 31.8 %copy-start.12 = (f32[35,1,256]{2,1,0:T(1,128)}, f32[35,1,256]{2,1,0:T(1,128)S(1)}, u32[]{:S(2)}) copy-start(f32[35,1,256]{2,1,0:T(1,128)S(1)} %collective-permute-done.2) | copy-start | bytes 107524
  208.4 31.3 %copy-start.14 = (f32[35,1,256]{2,1,0:T(1,128)}, f32[35,1,256]{2,1,0:T(1,128)S(1)}, u32[]{:S(2)}) copy-start(f32[35,1,256]{2,1,0:T(1,128)S(1)} %collective-permute-done.1) | copy-start | bytes 107524
  210.7 11.6 %copy-start.6 = (bf16[32,64,256]{2,1,0:T(8,128)(2,1)S(1)}, bf16[32,64,256]{2,1,0:T(8,128)(2,1)}, u32[]{:S(2)}) copy-start(bf16[32,64,256]{2,1,0:T(8,128)(2,1)} %param.19) | copy-start | bytes 3145732
  212.6 22.9 %collective-permute-start.3 = (f32[35,66,1]{1,2,0:T(1,128)S(1)}, f32[35,66,1]{1,2,0:T(1,128)S(1)}, u32[]{:S(2)}, u32[]{:S(2)}) collective-permute-start(f32[35,66,1]{1,2,0:T(1,128)S(1)} %copy.35), channel_id=1, source_target_pairs={{0,1},{1,2},{2,3},{3,4},{4,5},{5,6},{6,7},{7,8},{8,9},{9,10},{10,1... | collective-permute-start | bytes 27728 | tf_op jit(solution)/shard_map/ppermute | solution.py:32
  216.7 20.4 %collective-permute-start.4 = (f32[35,66,1]{1,2,0:T(1,128)S(1)}, f32[35,66,1]{1,2,0:T(1,128)S(1)}, u32[]{:S(2)}, u32[]{:S(2)}) collective-permute-start(f32[35,66,1]{1,2,0:T(1,128)S(1)} %copy.36), channel_id=1, source_target_pairs={{1,0},{2,1},{3,2},{4,3},{5,4},{6,5},{7,6},{8,7},{9,8},{10,9},{11,1... | collective-permute-start | bytes 27728 | tf_op jit(solution)/shard_map/ppermute | solution.py:33
  227.9 7.1 %copy-start.29 = (f32[32]{0:T(128)S(1)}, f32[32]{0:T(128)}, u32[]{:S(2)}) copy-start(f32[32]{0:T(128)} %param.25) | copy-start | bytes 388
  238.7 1.3 copy-start.3
  238.7 1.7 copy-start.5
  240.4 0.8 copy-start.25
  256.8 3.3 copy-start.7
  256.8 6.4 %copy-start.17 = (f32[2,64,256]{2,1,0:T(8,128)S(1)}, f32[2,64,256]{2,1,0:T(8,128)}, u32[]{:S(2)}) copy-start(f32[2,64,256]{2,1,0:T(8,128)} %param.20) | copy-start | bytes 393220
  256.8 6.4 %copy-start.18 = (f32[2,64,256]{2,1,0:T(8,128)S(1)}, f32[2,64,256]{2,1,0:T(8,128)}, u32[]{:S(2)}) copy-start(f32[2,64,256]{2,1,0:T(8,128)} %param.21) | copy-start | bytes 393220
  256.8 6.4 %copy-start.10 = (s32[64,256]{1,0:T(8,128)S(1)}, s32[64,256]{1,0:T(8,128)}, u32[]{:S(2)}) copy-start(s32[64,256]{1,0:T(8,128)} %param.22) | copy-start | bytes 196612
  256.9 6.3 %collective-permute-start.5 = (f32[64,256]{1,0:T(8,128)S(1)}, f32[64,256]{1,0:T(8,128)S(1)}, u32[]{:S(2)}, u32[]{:S(2)}) collective-permute-start(f32[64,256]{1,0:T(8,128)S(1)} %slice_bitcast_fusion.3), channel_id=1, source_target_pairs={{64,0},{128,64},{192,128},{65,1},{129,65},{193,129},{66,2},{130,66... | collective-permute-start | bytes 196616 | tf_op jit(solution)/shard_map/ppermute | solution.py:22
  263.2 6.0 %copy-start.16 = (f32[64,256]{1,0:T(8,128)}, f32[64,256]{1,0:T(8,128)S(1)}, u32[]{:S(2)}) copy-start(f32[64,256]{1,0:T(8,128)S(1)} %collective-permute-done.5) | copy-start | bytes 196612
  263.3 33.1 %copy-start.1 = (f32[35,64,256]{2,1,0:T(8,128)}, f32[35,64,256]{2,1,0:T(8,128)S(1)}, u32[]{:S(2)}) copy-start(f32[35,64,256]{2,1,0:T(8,128)S(1)} %bitcast_dynamic-update-slice_fusion) | copy-start | bytes 6881284
  263.3 16.9 %collective-permute-start.7 = (f32[35,1,256]{2,1,0:T(1,128)S(1)}, f32[35,1,256]{2,1,0:T(1,128)S(1)}, u32[]{:S(2)}, u32[]{:S(2)}) collective-permute-start(f32[35,1,256]{2,1,0:T(1,128)S(1)} %get-tuple-element.15), channel_id=1, source_target_pairs={{16,0},{32,16},{48,32},{17,1},{33,17},{49,33},{18,2},{34,18},{50,3... | collective-permute-start | bytes 107528 | tf_op jit(solution)/shard_map/ppermute | solution.py:33
  264.6 15.6 %collective-permute-start.6 = (f32[35,1,256]{2,1,0:T(1,128)S(1)}, f32[35,1,256]{2,1,0:T(1,128)S(1)}, u32[]{:S(2)}, u32[]{:S(2)}) collective-permute-start(f32[35,1,256]{2,1,0:T(1,128)S(1)} %get-tuple-element.14), channel_id=1, source_target_pairs={{0,16},{16,32},{32,48},{1,17},{17,33},{33,49},{2,18},{18,34},{34,5... | collective-permute-start | bytes 107528 | tf_op jit(solution)/shard_map/ppermute | solution.py:32
  280.3 16.1 %copy-start.11 = (f32[35,1,256]{2,1,0:T(1,128)}, f32[35,1,256]{2,1,0:T(1,128)S(1)}, u32[]{:S(2)}) copy-start(f32[35,1,256]{2,1,0:T(1,128)S(1)} %collective-permute-done.7) | copy-start | bytes 107524
  280.3 16.1 %copy-start.13 = (f32[35,1,256]{2,1,0:T(1,128)}, f32[35,1,256]{2,1,0:T(1,128)S(1)}, u32[]{:S(2)}) copy-start(f32[35,1,256]{2,1,0:T(1,128)S(1)} %collective-permute-done.6) | copy-start | bytes 107524
  284.3 7.9 %collective-permute-start.8 = (f32[35,66,1]{1,2,0:T(1,128)S(1)}, f32[35,66,1]{1,2,0:T(1,128)S(1)}, u32[]{:S(2)}, u32[]{:S(2)}) collective-permute-start(f32[35,66,1]{1,2,0:T(1,128)S(1)} %copy.42), channel_id=1, source_target_pairs={{0,1},{1,2},{2,3},{3,4},{4,5},{5,6},{6,7},{7,8},{8,9},{9,10},{10,1... | collective-permute-start | bytes 27728 | tf_op jit(solution)/shard_map/ppermute | solution.py:32
  288.0 5.7 %collective-permute-start.9 = (f32[35,66,1]{1,2,0:T(1,128)S(1)}, f32[35,66,1]{1,2,0:T(1,128)S(1)}, u32[]{:S(2)}, u32[]{:S(2)}) collective-permute-start(f32[35,66,1]{1,2,0:T(1,128)S(1)} %copy.43), channel_id=1, source_target_pairs={{1,0},{2,1},{3,2},{4,3},{5,4},{6,5},{7,6},{8,7},{9,8},{10,9},{11,1... | collective-permute-start | bytes 27728 | tf_op jit(solution)/shard_map/ppermute | solution.py:33
  295.3 1.3 copy-start.2
  295.3 1.7 copy-start.4
  297.1 0.8 copy-start.26
  297.9 37.0 %copy-start.21 = (f32[32]{0:T(128)S(1)}, f32[32]{0:T(128)}, u32[]{:S(2)}) copy-start(f32[32]{0:T(128)} %copy-done.20) | copy-start | bytes 388
  297.9 37.0 %copy-start.22 = (f32[32]{0:T(128)S(1)}, f32[32]{0:T(128)}, u32[]{:S(2)}) copy-start(f32[32]{0:T(128)} %param.28) | copy-start | bytes 388
  297.9 37.0 %copy-start.23 = (f32[32]{0:T(128)S(1)}, f32[32]{0:T(128)}, u32[]{:S(2)}) copy-start(f32[32]{0:T(128)} %param.27) | copy-start | bytes 388
  297.9 37.0 %copy-start.24 = (f32[32]{0:T(128)S(1)}, f32[32]{0:T(128)}, u32[]{:S(2)}) copy-start(f32[32]{0:T(128)} %param.26) | copy-start | bytes 388
Sparse Core Ops, SparseCore 0:
  15.2 49.6 all-reduce.6
  292.2 40.6 all-reduce.4
where the time goes:
time: 358 us; the launch traced here: 356 us
  blocking collectives  180 us (50%)
  local copies, waits for them, and re-layouts  51 us (14%)
  other arithmetic  42.6 us (12%)
  waiting for transfers between devices  38 us (11%)
  starting transfers between devices  26.4 us (7%)
  between operations  15.3 us (4%)
    unnamed x1, blocking collectives  126 us
    all_gather x1, blocking collectives, shards(): lax.all_gather(masked, ('lat', 'lon'), axis=0, tiled=True)  54.8 us
    psum x2, waiting for transfers between devices, from_root(): return lax.psum(kept, axis)  34.3 us
    add x2, other arithmetic, shards(): survive * after_move + recruit_term[None] * maturity[:, None, None]  27.9 us
    reshape x2, local copies, waits for them, and re-layouts, shards(): spread.reshape(ages_here, rows_y, rows_x)  14.1 us
    ppermute x4, starting transfers between devices, with_halo(): before = lax.ppermute(last, axis, up)  12.9 us
    ppermute x4, starting transfers between devices, with_halo(): after = lax.ppermute(first, axis, down)  10.7 us
    broadcast_in_dim x2, local copies, waits for them, and re-layouts, shards(): jnp.broadcast_to(block_grid[:, :, None, :, None], (ages_here, blocks_y, B...  7.82 us
  transfers between devices with their start and end apart: 12, of which 3 were waited for; matrix products, arithmetic and copies ran while one was open for 16% of the time, Pallas kernels for 0%

commit v1 on v0

v1 whole, which is shorter than its diff:
```python
import functools
import jax
import jax.numpy as jnp
from jax import lax
from jax.experimental import pallas as pl
from jax.experimental.pallas import tpu as pltpu
from jax.sharding import PartitionSpec as P

MESH = pl.DeviceIdType.MESH
HIGHEST = lax.Precision.HIGHEST
F32 = jnp.float32
I32 = jnp.int32

AGES = 32
ROWS = 64
LANES = 128
BY = 16
SLOTS = 8
CODE = 64
TOP = 8
FIRST_AGE = 8
FIELD_LANE = 66


def iota(shape, dim):
    return lax.broadcasted_iota(I32, shape, dim)


def as_column(row):
    n = row.shape[1]
    eye = iota((n, n), 0) == iota((n, n), 1)
    return jnp.sum(jnp.where(eye, jnp.broadcast_to(row, (n, n)), 0.0), axis=1, keepdims=True)


def as_row(column):
    n = column.shape[0]
    eye = iota((n, n), 0) == iota((n, n), 1)
    return jnp.sum(jnp.where(eye, jnp.broadcast_to(column, (n, n)), 0.0), axis=0, keepdims=True)


def kernel(
    sizes,
    saved, final, prey, heat, sea_in, fish, offspring,
    death, gear, spread, drift, level, breed,
    gear_v, spread_v, drift_v, level_v,
    landing, east, north, patch, bounds,
    out, grad,
    saved_v, final_v, adj1, adj0, rest, surv, hab,
    forage, warm, sea, open_e, open_s, rec,
    row_n1, row_s1, row_n0, row_s0,
    halo_n1, halo_s1, halo_n0, halo_s0,
    diag_n1, diag_s1, diag_n0, diag_s0,
    col1, col0, col_w1, col_e1, col_w0, col_e0,
    dcol_w1, dcol_e1, dcol_w0, dcol_e0,
    fix_col, fix_n, fix_s,
    first1, first0, spawn, spawn_in,
    catch_v, catch_out, catch_in, fold_out, fold_in, blocks,
    local_sem, send_sem, recv_sem,
):
    n_coh, n_lat, n_lon = sizes
    c, i, j = lax.axis_index("coh"), lax.axis_index("lat"), lax.axis_index("lon")
    c_up, c_dn = lax.rem(c + 1, n_coh), lax.rem(c + n_coh - 1, n_coh)
    i_up, i_dn = lax.rem(i + 1, n_lat), lax.rem(i + n_lat - 1, n_lat)
    j_up, j_dn = lax.rem(j + 1, n_lon), lax.rem(j + n_lon - 1, n_lon)
    total_ages = AGES * n_coh

    def at(cc, ii, jj):
        return {"coh": cc, "lat": ii, "lon": jj}

    load_final = pltpu.make_async_copy(final, final_v, local_sem.at[0])
    load_saved = [pltpu.make_async_copy(saved.at[t], saved_v.at[t], local_sem.at[1 + t]) for t in range(2)]
    load_final.start()
    load_saved[1].start()
    load_saved[0].start()

    barrier = pltpu.get_barrier_semaphore()
    partners = [at(c, i, lax.rem(j + d, n_lon)) for d in range(1, n_lon)]
    partners += [at(c, lax.rem(i + d, n_lat), j) for d in range(1, n_lat)]
    partners += [at(lax.rem(c + d, n_coh), i, j) for d in range(1, n_coh)]
    partners += [at(cc, ii, j) for cc in (c_up, c_dn) for ii in (i_up, i_dn)]
    partners += [at(cc, i, jj) for cc in (c_up, c_dn) for jj in (j_up, j_dn)]
    for partner in partners:
        pl.semaphore_signal(barrier, inc=1, device_id=partner, device_id_type=MESH)

    def remote(src, dst, k, to):
        return pltpu.make_async_remote_copy(
            src_ref=src, dst_ref=dst, send_sem=send_sem.at[k], recv_sem=recv_sem.at[k],
            device_id=to, device_id_type=MESH,
        )

    lane = iota((BY, LANES), 1)
    lane_all = iota((ROWS, LANES), 1)
    age_lane = ((lane + 1) & 127) >> 1
    age_lane_all = ((lane_all + 1) & 127) >> 1
    even_all = (lane_all & 1) == 0

    def mature(a):
        return (c * AGES + a + 1).astype(F32) * (1.0 / total_ages) * breed[a]

    east_col = east[...].astype(F32)
    east_row = as_row(east_col)
    same = jnp.broadcast_to(east_col, (32, 32)) == jnp.broadcast_to(east_row, (32, 32))
    ahead = same & (iota((32, 32), 0) < iota((32, 32), 1))
    rank_row = jnp.sum(jnp.where(ahead, 1.0, 0.0), axis=0, keepdims=True)
    slot_row = east_row * SLOTS + rank_row
    code_col = as_column((north[...] * 32 + patch[...]).astype(F32))
    cohort = c * AGES + iota((32, AGES), 1)
    inside = (cohort >= bounds[:, 0:1]) & (cohort < bounds[:, 1:2])
    catch_v[...] = jnp.broadcast_to(code_col, (32, LANES))
    catch_v[:, 0:32] = jnp.where(inside, landing[:, 0, :], 0.0)
    catch_v[:, 32:64] = jnp.where(inside, landing[:, 1, :], 0.0)
    slots = n_lon * SLOTS
    place = jnp.where(iota((slots, 32), 0).astype(F32) == jnp.broadcast_to(slot_row, (slots, 32)), 1.0, 0.0)
    placed = jnp.dot(place, catch_v[...], precision=HIGHEST, preferred_element_type=F32)
    catch_out[...] = placed.reshape(n_lon, SLOTS, LANES)
    catch_in[j] = catch_out[j]

    def halves(h):
        return slice(h * LANES, (h + 1) * LANES)

    body = slice(TOP, TOP + ROWS)
    for h in range(2):
        sea[h] = sea_in[:, halves(h)].astype(F32)
    last_lane = lane_all == LANES - 1
    sea0, sea1 = sea[0], sea[1]
    next0 = jnp.where(last_lane, pltpu.roll(sea1, LANES - 1, 1), pltpu.roll(sea0, LANES - 1, 1))
    next1 = jnp.where(last_lane, 0.0, pltpu.roll(sea1, LANES - 1, 1))
    open_e[0] = sea0 * next0
    open_e[1] = sea1 * next1
    last_row = iota((ROWS, LANES), 0) == ROWS - 1
    for h, here in enumerate((sea0, sea1)):
        below = jnp.where(last_row, 0.0, pltpu.roll(here, ROWS - 1, 0))
        open_s[h, 0:TOP, :] = jnp.zeros((TOP, LANES), F32)
        open_s[h, body, :] = here * below
        hab[h, 0:TOP, :] = jnp.zeros((TOP, LANES), F32)
        hab[h, TOP + ROWS:, :] = jnp.zeros((TOP, LANES), F32)
    for t in range(2):
        for h, here in enumerate((sea0, sea1)):
            forage[t, h] = here * prey[t, :, halves(h)]
            warm[t, h] = heat[t, :, halves(h)] * 0.25

    def field(f, h):
        if f == 4:
            return sea[h]
        return (forage, warm)[f % 2][1 - f // 2, h]

    columns = jnp.zeros((ROWS, LANES), F32)
    for h in range(2):
        row_n1[h, 0:8, :] = jnp.zeros((8, LANES), F32)
        row_s1[h, 0:8, :] = jnp.zeros((8, LANES), F32)
    for f in range(5):
        for h in range(2):
            plane = field(f, h)
            row_n1[h, f:f + 1, :] = plane[0:1]
            row_s1[h, f:f + 1, :] = plane[ROWS - 1:ROWS]
        columns = jnp.where(lane_all == FIELD_LANE + 2 * f, jnp.broadcast_to(field(f, 0)[:, 0:1], (ROWS, LANES)), columns)
        columns = jnp.where(
            lane_all == FIELD_LANE + 2 * f + 1, jnp.broadcast_to(field(f, 1)[:, LANES - 1:], (ROWS, LANES)), columns
        )
    col0[...] = jnp.zeros((ROWS, LANES), F32)

    pad = jnp.zeros((TOP, LANES), F32)

    def clear_pads(adj, a):
        for h in range(2):
            adj[a, h, 0:TOP, :] = pad
            adj[a, h, TOP + ROWS:, :] = pad

    def pick_columns(a, x0, x1):
        width = iota(x0.shape, 1)
        edges = jnp.where(width == 0, x0, x1)
        return ((width + 1) & 127) >> 1 == a, pltpu.roll(edges, 2 * a, 1)

    load_final.wait()

    def unpack(a, columns):
        x = final_v[a].astype(F32)
        x0, x1 = x[:, :LANES], x[:, LANES:]
        clear_pads(adj1, a)
        clear_pads(adj0, a)
        for h, xh in enumerate((x0, x1)):
            adj1[a, h, body, :] = xh
            row_n1[h, pl.ds(FIRST_AGE + a, 1), :] = xh[0:1]
            row_s1[h, pl.ds(FIRST_AGE + a, 1), :] = xh[ROWS - 1:]
        mine, moved = pick_columns(a, x0, x1)
        return jnp.where(mine, moved, columns)

    col1[...] = lax.fori_loop(0, AGES, unpack, columns)
    clear_pads(adj1, AGES)
    clear_pads(adj0, AGES)

    def spawn_part(t):
        def add(a, total):
            return total + mature(a) * saved_v[t, a].astype(F32)

        total = lax.fori_loop(0, AGES, add, jnp.zeros((ROWS, 2 * LANES), F32))
        for h in range(2):
            spawn[t, h] = total[:, halves(h)]

    load_saved[1].wait()
    spawn_part(1)

    pl.semaphore_wait(barrier, len(partners))

    catch_sends = [
        remote(catch_out.at[lax.rem(j + d, n_lon)], catch_in.at[j], d, at(c, i, lax.rem(j + d, n_lon)))
        for d in range(1, n_lon)
    ]
    for copy in catch_sends:
        copy.start()

    k_fold, k_spawn, k_month = 16, 20, 28

    def spawn_copies(t):
        return [
            remote(spawn.at[t], spawn_in.at[t, d - 1], k_spawn + 4 * t + d, at(lax.rem(c + d, n_coh), i, j))
            for d in range(1, n_coh)
        ]

    def month_copies(t):
        k = k_month + 12 * (1 - t)
        adj = (adj0, adj1)[t]
        col = (col0, col1)[t]
        span = slice(0, 40) if t == 1 else slice(FIRST_AGE, 40)
        row_n, row_s = ((row_n0, row_s0), (row_n1, row_s1))[t]
        halo_n, halo_s = ((halo_n0, halo_s0), (halo_n1, halo_s1))[t]
        diag_n, diag_s = ((diag_n0, diag_s0), (diag_n1, diag_s1))[t]
        col_w, col_e = ((col_w0, col_e0), (col_w1, col_e1))[t]
        dcol_w, dcol_e = ((dcol_w0, dcol_e0), (dcol_w1, dcol_e1))[t]
        first = (first0, first1)[t]
        side = [
            remote(row_n.at[:, span, :], halo_s.at[:, span, :], k, at(c, i_dn, j)),
            remote(row_s.at[:, span, :], halo_n.at[:, span, :], k + 1, at(c, i_up, j)),
            remote(col, col_e, k + 4, at(c, i, j_dn)),
            remote(col, col_w, k + 5, at(c, i, j_up)),
        ]
        younger = [
            remote(adj.at[0, :, body, :], adj.at[AGES, :, body, :], k + 8, at(c_dn, i, j)),
            remote(adj.at[0, :, TOP:TOP + 8, :], diag_s, k + 2, at(c_dn, i_dn, j)),
            remote(adj.at[0, :, TOP + ROWS - 8:TOP + ROWS, :], diag_n, k + 3, at(c_dn, i_up, j)),
            remote(col, dcol_e, k + 6, at(c_dn, i, j_dn)),
            remote(col, dcol_w, k + 7, at(c_dn, i, j_up)),
        ]
        root = [remote(adj.at[0, :, body, :], first, k + 8 + d, at(d, i, j)) for d in range(1, n_coh)]
        return side, younger, root

    def start_month(t):
        side, younger, root = month_copies(t)
        adj, first = (adj0, adj1)[t], (first0, first1)[t]

        @pl.when(c > 0)
        def _():
            younger[0].start()

        @pl.when(c == 0)
        def _():
            for copy in root:
                copy.start()
            for h in range(2):
                first[h] = adj[0, h, body, :]

        for copy in side:
            copy.start()

        @pl.when(c > 0)
        def _():
            for copy in younger[1:]:
                copy.start()

    start_month(1)
    for copy in spawn_copies(1):
        copy.start()
    load_saved[0].wait()
    spawn_part(0)
    for copy in spawn_copies(0):
        copy.start()

    def interior(t, adj, a):
        spread_a, drift_a, level_a = spread[a], drift[a], level[a] * 0.25
        for h in range(2):
            for r in range(0, ROWS, BY):
                rows = slice(r, r + BY)
                q = warm[t, h, rows, :] - level_a
                hab[h, TOP + r:TOP + r + BY, :] = forage[t, h, rows, :] * drift_a / (1.0 + q * q)
                if t == 1:
                    surv[a, h, rows, :] = jnp.exp(-death[a] - gear[a] * fish[rows, halves(h)])
        for r in range(0, ROWS, BY):
            rows = slice(r, r + BY)
            mid, up, dn = (slice(TOP + r + s, TOP + r + s + BY) for s in (0, -1, 1))
            h0, h1 = hab[0, mid, :], hab[1, mid, :]
            l0, l1 = adj[a + 1, 0, mid, :], adj[a + 1, 1, mid, :]
            turn = LANES - 1
            hr1, lr1 = pltpu.roll(h1, turn, 1), pltpu.roll(l1, turn, 1)
            hr0 = jnp.where(lane == turn, hr1, pltpu.roll(h0, turn, 1))
            lr0 = jnp.where(lane == turn, lr1, pltpu.roll(l0, turn, 1))
            kept, given = [], []
            for h, hh, ll, hr, lr in ((0, h0, l0, hr0, lr0), (1, h1, l1, hr1, lr1)):
                g = hr - hh
                k = jnp.maximum(g, 0.0) + spread_a
                o = open_e[h, rows, :] * (ll - lr)
                y = ll - k * o
                given.append((k - g) * o)
                for shift, gate in ((up, up), (dn, mid)):
                    k = jnp.maximum(hab[h, shift, :] - hh, 0.0) + spread_a
                    y = y - k * (open_s[h, gate, :] * (ll - adj[a + 1, h, shift, :]))
                kept.append(y)
            m0, m1 = pltpu.roll(given[0], 1, 1), pltpu.roll(given[1], 1, 1)
            rest[a, 0, rows, :] = kept[0] + jnp.where(lane == 0, m1, m0)
            rest[a, 1, rows, :] = kept[1] + jnp.where(lane == 0, m0, m1)

    def interiors(t, lo, hi):
        adj = (adj0, adj1)[t]

        def step(a, carry):
            interior(t, adj, a)
            return carry

        lax.fori_loop(lo, hi, step, 0)

    age_of = iota((AGES, LANES), 0)
    lane_age = ((iota((AGES, LANES), 1) + 1) & 127) >> 1

    def by_row(v):
        return as_column(v[...])

    def by_lane(v):
        wide = jnp.broadcast_to(by_row(v), (AGES, LANES))
        return jnp.sum(jnp.where(age_of == lane_age, wide, 0.0), axis=0, keepdims=True)

    north_open = jnp.where(i > 0, 1.0, 0.0)
    south_open = jnp.where(i < n_lat - 1, 1.0, 0.0)
    west_open = jnp.where(j > 0, 1.0, 0.0)
    east_open = jnp.where(j < n_lon - 1, 1.0, 0.0)

    def edges(t):
        adj = (adj0, adj1)[t]
        side, younger, root = month_copies(t)
        halo_n, halo_s = ((halo_n0, halo_s0), (halo_n1, halo_s1))[t]
        row_n, row_s = ((row_n0, row_s0), (row_n1, row_s1))[t]
        diag_n, diag_s = ((diag_n0, diag_s0), (diag_n1, diag_s1))[t]
        col = (col0, col1)[t]
        col_w, col_e = ((col_w0, col_e0), (col_w1, col_e1))[t]
        dcol_w, dcol_e = ((dcol_w0, dcol_e0), (dcol_w1, dcol_e1))[t]
        for copy in side:
            copy.wait_recv()

        @pl.when(c < n_coh - 1)
        def _():
            for copy in younger[1:]:
                copy.wait_recv()

        @pl.when(c == n_coh - 1)
        def _():
            diag_n[...] = jnp.zeros_like(diag_n)
            diag_s[...] = jnp.zeros_like(diag_s)
            dcol_w[...] = jnp.zeros_like(dcol_w)
            dcol_e[...] = jnp.zeros_like(dcol_e)

        past = FIRST_AGE + AGES
        for h in range(2):
            row_n[h, past:past + 1, :] = adj[AGES, h, TOP:TOP + 1, :]
            row_s[h, past:past + 1, :] = adj[AGES, h, TOP + ROWS - 1:TOP + ROWS, :]
            halo_n[h, past:past + 1, :] = diag_n[h, 7:8, :]
            halo_s[h, past:past + 1, :] = diag_s[h, 0:1, :]
        later = slice(FIRST_AGE + 1, FIRST_AGE + 1 + AGES)
        f = 2 * (1 - t)
        spread_r, drift_r, level_r = (
            jnp.broadcast_to(x, (AGES, LANES)) for x in (by_row(spread_v), by_row(drift_v), by_row(level_v) * 0.25)
        )
        for own, halo, own1, halo1, gate, fix in (
            (row_n, halo_n, row_n1, halo_n1, north_open, fix_n),
            (row_s, halo_s, row_s1, halo_s1, south_open, fix_s),
        ):
            for h in range(2):
                def habitat(buf):
                    q = buf[h, f + 1:f + 2, :] - level_r
                    return buf[h, f:f + 1, :] * drift_r / (1.0 + q * q)

                passage = own1[h, 4:5, :] * halo1[h, 4:5, :] * gate
                k = spread_r + jnp.maximum(habitat(halo1) - habitat(own1), 0.0)
                fix[h] = passage * k * (own[h, later, :] - halo[h, later, :])

        def both(own_w, own_e):
            wide = (ROWS, LANES)
            return jnp.where(even_all, jnp.broadcast_to(own_w, wide), jnp.broadcast_to(own_e, wide))

        def own_field(f):
            return both(field(f, 0)[:, 0:1], field(f, 1)[:, LANES - 1:])

        def halo_field(f):
            spot = FIELD_LANE + 2 * f
            return both(col_w1[:, spot + 1:spot + 2], col_e1[:, spot:spot + 1])

        spread_l, drift_l, level_l = (by_lane(x) for x in (spread_v, drift_v, level_v))

        def habitat_columns(get):
            q = get(f + 1) - level_l * 0.25
            return get(f) * drift_l / (1.0 + q * q)

        passage = own_field(4) * halo_field(4) * jnp.where(even_all, west_open, east_open)
        mine, moved = pick_columns(AGES, adj[AGES, 0, body, :], adj[AGES, 1, body, :])
        own = pltpu.roll(jnp.where(mine, moved, col[...]), LANES - 2, 1)
        other = jnp.where(even_all, pltpu.roll(col_w[...], LANES - 1, 1), pltpu.roll(col_e[...], LANES - 3, 1))
        other = jnp.where(lane_all == 62, pltpu.roll(dcol_w[...], 63, 1), other)
        other = jnp.where(lane_all == 61, pltpu.roll(dcol_e[...], 61, 1), other)
        k = spread_l + jnp.maximum(habitat_columns(halo_field) - habitat_columns(own_field), 0.0)
        fix_col[...] = passage * k * (own - other)

    def finish(t):
        adj_next = adj0
        place = t * AGES

        def step(a, carry):
            scale = mature(a)
            for h in range(2):
                rest[a, h, 0:1, :] = rest[a, h, 0:1, :] - fix_n[h, pl.ds(a, 1), :]
                rest[a, h, ROWS - 1:ROWS, :] = rest[a, h, ROWS - 1:ROWS, :] - fix_s[h, pl.ds(a, 1), :]
            for b in range(ROWS // BY):
                rows = slice(b * BY, (b + 1) * BY)
                turned = pltpu.roll(fix_col[rows, :], (LANES - 2 * a) & (LANES - 1), 1)
                made = []
                for h in range(2):
                    spot = (0, LANES - 1)[h]
                    moved = rest[a, h, rows, :] - jnp.where(lane == spot, turned, 0.0)
                    caught = jnp.broadcast_to(blocks[2 * b + h, pl.ds(place + a, 1), :], (BY, LANES))
                    made.append(
                        surv[a, h, rows, :] * moved + rec[h, rows, :] * scale + fish[rows, halves(h)] * caught
                    )
                if t == 1:
                    for h in range(2):
                        adj_next[a, h, TOP + b * BY:TOP + (b + 1) * BY, :] = made[h]
                        if b == 0:
                            row_n0[h, pl.ds(FIRST_AGE + a, 1), :] = made[h][0:1]
                        if b == ROWS // BY - 1:
                            row_s0[h, pl.ds(FIRST_AGE + a, 1), :] = made[h][BY - 1:]
                    mine, moved = pick_columns(a, made[0], made[1])
                    col0[rows, :] = jnp.where(mine, moved, col0[rows, :])
                else:
                    for h in range(2):
                        out[a, rows, halves(h)] = made[h]
            return carry

        lax.fori_loop(0, AGES, step, 0)

    def last_cohort(t):
        adj = (adj0, adj1)[t]
        side, younger, root = month_copies(t)

        @pl.when(c < n_coh - 1)
        def _():
            younger[0].wait_recv()

        @pl.when(c == n_coh - 1)
        def _():
            for h in range(2):
                adj[AGES, h, body, :] = jnp.zeros((ROWS, LANES), F32)

        interiors(t, AGES - 1, AGES)

    def recruit(t):
        first = (first0, first1)[t]
        side, younger, root = month_copies(t)
        for d in range(1, n_coh):
            @pl.when(c == d)
            def _():
                root[d - 1].wait_recv()
        for copy in spawn_copies(t):
            copy.wait_recv()
        for h in range(2):
            total = spawn[t, h]
            for d in range(1, n_coh):
                total = total + spawn_in[t, d - 1, h]
            ratio = 1.0 / (1.0 + total)
            base = first[h] * sea[h]
            rec[h] = base * offspring[:, halves(h)] * ratio * ratio
            gain = base * total * ratio
            if t == 1:
                grad[:, halves(h)] = gain
            else:
                grad[:, halves(h)] = grad[:, halves(h)] + gain

    fold_sends = [
        remote(fold_out.at[lax.rem(i + d, n_lat)], fold_in.at[i], k_fold + d, at(c, lax.rem(i + d, n_lat), j))
        for d in range(1, n_lat)
    ]

    interiors(1, 0, AGES // 2)
    for copy in catch_sends:
        copy.wait_recv()
    got = catch_in[...].reshape(slots, LANES)
    codes = n_lat * 32
    code_row = as_row(got[:, CODE:CODE + 1])
    pick = jnp.where(iota((codes, slots), 0).astype(F32) == jnp.broadcast_to(code_row, (codes, slots)), 1.0, 0.0)
    folded = jnp.dot(pick, got, precision=HIGHEST, preferred_element_type=F32)
    fold_out[...] = folded.reshape(n_lat, 32, LANES)
    fold_in[i] = fold_out[i]
    for copy in fold_sends:
        copy.start()
    interiors(1, AGES // 2, AGES - 1)
    last_cohort(1)
    edges(1)
    recruit(1)
    for copy in fold_sends:
        copy.wait_recv()
    block = fold_in[0]
    for d in range(1, n_lat):
        block = block + fold_in[d]
    cells = 2 * LANES * (ROWS // BY)
    widen = jnp.where(iota((32, cells), 0) == iota((32, cells), 1) >> 5, 1.0, 0.0)
    planes = lax.dot_general(block, widen, (((0,), (0,)), ((), ())), precision=HIGHEST, preferred_element_type=F32)
    gear_r = jnp.broadcast_to(by_row(gear_v), (AGES, LANES))
    for b in range(cells // LANES):
        for t in range(2):
            blocks[b, t * AGES:(t + 1) * AGES, :] = (
                planes[t * AGES:(t + 1) * AGES, b * LANES:(b + 1) * LANES] * gear_r
            )
    finish(1)
    start_month(0)
    interiors(0, 0, AGES - 1)
    last_cohort(0)
    edges(0)
    recruit(0)
    finish(0)

    for copy in catch_sends + fold_sends + spawn_copies(1) + spawn_copies(0):
        copy.wait_send()
    for t in range(2):
        side, younger, root = month_copies(t)
        for copy in side:
            copy.wait_send()

        @pl.when(c > 0)
        def _():
            for copy in younger:
                copy.wait_send()

        @pl.when(c == 0)
        def _():
            for copy in root:
                copy.wait_send()


def shards(
    sizes,
    saved, final, prey, heat, sea, fish, offspring,
    death, gear, spread, drift, level, breed,
    landing, east, north, patch, bounds,
):
    n_coh, n_lat, n_lon = sizes
    vmem = pl.BlockSpec(memory_space=pltpu.VMEM)
    smem = pl.BlockSpec(memory_space=pltpu.SMEM)
    anywhere = pl.BlockSpec(memory_space=pl.ANY)
    plane = (2, ROWS, LANES)
    padded = (AGES + 1, 2, ROWS + 2 * TOP, LANES)
    edge_rows, tile, column = (2, 48, LANES), (2, 8, LANES), (ROWS, LANES)

    def f32(shape):
        return pltpu.VMEM(shape, F32)

    scratch = [
        pltpu.VMEM((2, AGES, ROWS, 2 * LANES), jnp.bfloat16),
        pltpu.VMEM((AGES, ROWS, 2 * LANES), jnp.bfloat16),
        f32(padded), f32(padded),
        f32((AGES, *plane)), f32((AGES, *plane)),
        f32((2, ROWS + 2 * TOP, LANES)),
        f32((2, *plane)), f32((2, *plane)),
        f32(plane), f32(plane), f32((2, ROWS + 2 * TOP, LANES)), f32(plane),
        *[f32(edge_rows) for _ in range(8)],
        *[f32(tile) for _ in range(4)],
        *[f32(column) for _ in range(10)],
        f32(column), f32((2, AGES, LANES)), f32((2, AGES, LANES)),
        f32(plane), f32(plane),
        f32((2, *plane)), f32((2, n_coh - 1, *plane)),
        f32((32, LANES)), f32((n_lon, SLOTS, LANES)), f32((n_lon, SLOTS, LANES)),
        f32((n_lat, 32, LANES)), f32((n_lat, 32, LANES)),
        f32((2 * ROWS // BY, 2 * AGES, LANES)),
        pltpu.SemaphoreType.DMA((3,)),
        pltpu.SemaphoreType.DMA((52,)),
        pltpu.SemaphoreType.DMA((52,)),
    ]
    return pl.pallas_call(
        functools.partial(kernel, sizes),
        out_shape=(
            jax.ShapeDtypeStruct((AGES, ROWS, 2 * LANES), F32),
            jax.ShapeDtypeStruct((ROWS, 2 * LANES), F32),
        ),
        in_specs=[anywhere] * 2 + [vmem] * 5 + [smem] * 6 + [vmem] * 9,
        out_specs=(vmem, vmem),
        scratch_shapes=scratch,
        compiler_params=pltpu.CompilerParams(
            collective_id=0, has_side_effects=True, vmem_limit_bytes=48 * 1024 * 1024
        ),
    )(
        saved, final, prey, heat, sea, fish, offspring,
        death, gear, spread, drift, level, breed,
        gear.reshape(1, -1), spread.reshape(1, -1), drift.reshape(1, -1), level.reshape(1, -1),
        landing, east, north.reshape(1, -1), patch.reshape(1, -1), bounds,
    )


def solution(mesh):
    sizes = tuple(mesh.shape[axis] for axis in ("coh", "lat", "lon"))
    tile = P("lat", "lon")
    months = P(None, "lat", "lon")
    rows = ("lat", "lon")
    in_specs = (
        P(None, "coh", "lat", "lon"), P("coh", "lat", "lon"), months, months, tile, tile, tile,
        *[P("coh")] * 6,
        P(rows, None, "coh"), P(rows, None), P(rows), P(rows), P(rows, None),
    )
    out_specs = (P("coh", "lat", "lon"), tile)
    return jax.shard_map(
        functools.partial(shards, sizes), mesh=mesh, in_specs=in_specs, out_specs=out_specs, check_vma=False
    )
```

time: 358 us -> 53.8 us (0.15)
  blocking collectives: 180 us -> 0 us
  other arithmetic: 42.6 us -> 0 us
  waiting for transfers between devices: 38 us -> 0 us
  Pallas kernels: 0 us -> 36.1 us
  local copies, waits for them, and re-layouts: 51 us -> 16.6 us
  starting transfers between devices: 26.4 us -> 0 us
  between operations: 15.3 us -> 0.66 us
    unnamed x1 -> x0, blocking collectives: 126 us -> none
    all_gather x1 -> x0, blocking collectives: 54.8 us -> none  [shards(): lax.all_gather(masked, ('lat', 'lon'), axis=0, tiled=True)]
    pallas_call x0 -> x1, Pallas kernels: none -> 36.1 us  [shards(): pl.pallas_call(functools.partial(kernel, sizes), out_shape=(jax.ShapeDtyp...]
    psum x2 -> x0, waiting for transfers between devices: 34.3 us -> none  [from_root(): return lax.psum(kept, axis)]
    add x4 -> x0, other arithmetic: 29.8 us -> none  [the longest x2 27.9 us: shards(): survive * after_move + recruit_term[None] * maturity[:, None, None]]
    ppermute x10 -> x0, starting transfers between devices: 26.3 us -> none  [the longest x4 12.9 us: with_halo(): before = lax.ppermute(last, axis, up)]
    slice x10 -> x0, local copies, waits for them, and re-layouts: 14.5 us -> none  [the longest x4 7.35 us: with_halo(): first = lax.slice_in_dim(x, 0, width, axis=dim)]
    reshape x3 -> x0, local copies, waits for them, and re-layouts: 14.2 us -> none  [the longest x2 14.1 us: shards(): spread.reshape(ages_here, rows_y, rows_x)]
  transfers between devices with their start and end apart: 12 -> 0, of which waited for: 3 -> 0; matrix products, arithmetic and copies ran while one was open for 16% -> 0% of each run, Pallas kernels for 0% -> 0%
where the time goes in v1:
time: 53.8 us; the launch traced here: 53.3 us
  Pallas kernels  36.1 us (67%)
  local copies, waits for them, and re-layouts  16.6 us (31%)
  between operations  0.66 us (1%)
    pallas_call x1, Pallas kernels, shards(): pl.pallas_call(functools.partial(kernel, sizes), out_shape=(jax.ShapeDtyp...  36.1 us
    unnamed x36, local copies, waits for them, and re-layouts  16.6 us

profile of v1, /device:TPU:1, one launch (start us, length us, event | category | flops | bytes accessed | tf_op | source)
XLA Modules:
  0.0 53.3 jit_solution(7846293678852833144)
XLA Ops:
  0.6 0.7 %copy.20.east = s32[32,1]{1,0:T(8,128)S(1)} copy(s32[32,1]{0,1:T(1,128)} %param.32) | data formatting | bytes 256 | tf_op args[14]
  1.4 0.8 %copy.21.bounds = s32[32,2]{1,0:T(8,128)S(1)} copy(s32[32,2]{0,1:T(2,128)} %param.35) | data formatting | bytes 512 | tf_op args[17]
  2.1 0.0 copy-start
  2.1 1.6 %copy-done = bf16[2,32,64,256]{3,2,1,0:T(8,128)(2,1)S(1)} copy-done((bf16[2,32,64,256]{3,2,1,0:T(8,128)(2,1)S(1)}, bf16[2,32,64,256]{3,2,1,0:T(8,128)(2,1)}, u32[]{:S(2)}) %copy-start) | copy-done | bytes 2097176
  3.7 0.0 copy-start.1
  3.7 1.2 %copy-done.1 = bf16[32,64,256]{2,1,0:T(8,128)(2,1)S(1)} copy-done((bf16[32,64,256]{2,1,0:T(8,128)(2,1)S(1)}, bf16[32,64,256]{2,1,0:T(8,128)(2,1)}, u32[]{:S(2)}) %copy-start.1) | copy-done | bytes 1048600
  4.9 0.0 copy-start.2
  4.9 0.9 %copy-done.2 = f32[2,64,256]{2,1,0:T(8,128)S(1)} copy-done((f32[2,64,256]{2,1,0:T(8,128)S(1)}, f32[2,64,256]{2,1,0:T(8,128)}, u32[]{:S(2)}) %copy-start.2) | copy-done | bytes 131096
  5.8 0.0 copy-start.3
  5.8 0.9 %copy-done.3 = f32[2,64,256]{2,1,0:T(8,128)S(1)} copy-done((f32[2,64,256]{2,1,0:T(8,128)S(1)}, f32[2,64,256]{2,1,0:T(8,128)}, u32[]{:S(2)}) %copy-start.3) | copy-done | bytes 131096
  6.8 0.0 copy-start.4
  6.8 0.8 %copy-done.4 = s32[64,256]{1,0:T(8,128)S(1)} copy-done((s32[64,256]{1,0:T(8,128)S(1)}, s32[64,256]{1,0:T(8,128)}, u32[]{:S(2)}) %copy-start.4) | copy-done | bytes 65560
  7.6 0.0 copy-start.5
  7.6 0.8 %copy-done.5 = f32[64,256]{1,0:T(8,128)S(1)} copy-done((f32[64,256]{1,0:T(8,128)S(1)}, f32[64,256]{1,0:T(8,128)}, u32[]{:S(2)}) %copy-start.5) | copy-done | bytes 65560
  8.4 0.0 copy-start.6
  8.4 0.8 %copy-done.6 = f32[64,256]{1,0:T(8,128)S(1)} copy-done((f32[64,256]{1,0:T(8,128)S(1)}, f32[64,256]{1,0:T(8,128)}, u32[]{:S(2)}) %copy-start.6) | copy-done | bytes 65560
  9.3 0.0 copy-start.7
  9.3 0.8 %copy-done.7 = f32[32,2,32]{2,1,0:T(2,128)S(1)} copy-done((f32[32,2,32]{2,1,0:T(2,128)S(1)}, f32[32,2,32]{2,1,0:T(2,128)}, u32[]{:S(2)}) %copy-start.7) | copy-done | bytes 8216
  10.0 0.0 copy-start.8
  10.0 0.7 %copy-done.8 = f32[32]{0:T(128)S(1)} copy-done((f32[32]{0:T(128)S(1)}, f32[32]{0:T(128)}, u32[]{:S(2)}) %copy-start.8) | copy-done | bytes 152
  10.7 0.0 copy-start.9
  10.7 0.7 %copy-done.9 = f32[32]{0:T(128)S(1)} copy-done((f32[32]{0:T(128)S(1)}, f32[32]{0:T(128)}, u32[]{:S(2)}) %copy-start.9) | copy-done | bytes 152
  11.3 0.0 copy-start.10
  11.3 0.7 %copy-done.10 = f32[32]{0:T(128)S(1)} copy-done((f32[32]{0:T(128)S(1)}, f32[32]{0:T(128)}, u32[]{:S(2)}) %copy-start.10) | copy-done | bytes 152
  12.0 0.0 copy-start.11
  12.0 0.7 %copy-done.11 = f32[32]{0:T(128)S(1)} copy-done((f32[32]{0:T(128)S(1)}, f32[32]{0:T(128)}, u32[]{:S(2)}) %copy-start.11) | copy-done | bytes 152
  12.7 0.0 copy-start.12
  12.7 0.7 %copy-done.12 = f32[32]{0:T(128)S(1)} copy-done((f32[32]{0:T(128)S(1)}, f32[32]{0:T(128)}, u32[]{:S(2)}) %copy-start.12) | copy-done | bytes 152
  13.3 0.0 copy-start.13
  13.3 0.7 %copy-done.13 = f32[32]{0:T(128)S(1)} copy-done((f32[32]{0:T(128)S(1)}, f32[32]{0:T(128)}, u32[]{:S(2)}) %copy-start.13) | copy-done | bytes 152
  14.0 0.0 copy-start.14
  14.0 0.7 %copy-done.14 = s32[32]{0:T(128)S(1)} copy-done((s32[32]{0:T(128)S(1)}, s32[32]{0:T(128)}, u32[]{:S(2)}) %copy-start.14) | copy-done | bytes 152
  14.6 0.0 copy-start.15
  14.6 0.7 %copy-done.15 = s32[32]{0:T(128)S(1)} copy-done((s32[32]{0:T(128)S(1)}, s32[32]{0:T(128)}, u32[]{:S(2)}) %copy-start.15) | copy-done | bytes 152
  15.3 36.1 %shard_map.185 = (f32[32,64,256]{2,1,0:T(8,128)S(1)}, f32[64,256]{1,0:T(8,128)S(1)}) custom-call(bf16[2,32,64,256]{3,2,1,0:T(8,128)(2,1)S(1)} %copy-done, bf16[32,64,256]{2,1,0:T(8,128)(2,1)S(1)} %copy-done.1, f32[2,64,256]{2,1,0:T(8,128)S(1)} %copy-done.2, f32[2,64,256]{2,1,0:T(8,128)S(1)} %copy-done.3, s32[64,256]{1,0:T(8,128)S(1)} %copy-done.4, ...), custom_call_target="tpu_custom_call" | custom-call | tf_op jit(solution)/shard_map/pallas_call | solution.py:581
  51.4 1.3 %copy.24 = f32[32,64,256]{2,1,0:T(8,128)} copy(f32[32,64,256]{2,1,0:T(8,128)S(1)} %get-tuple-element.4) | data formatting | bytes 4194304
  52.7 0.6 %copy.25 = f32[64,256]{1,0:T(8,128)} copy(f32[64,256]{1,0:T(8,128)S(1)} %get-tuple-element.5) | data formatting | bytes 131072
Async XLA Ops:
  2.1 1.6 %copy-start = (bf16[2,32,64,256]{3,2,1,0:T(8,128)(2,1)S(1)}, bf16[2,32,64,256]{3,2,1,0:T(8,128)(2,1)}, u32[]{:S(2)}) copy-start(bf16[2,32,64,256]{3,2,1,0:T(8,128)(2,1)} %saved.1) | copy-start | bytes 6291460
  3.7 1.2 %copy-start.1 = (bf16[32,64,256]{2,1,0:T(8,128)(2,1)S(1)}, bf16[32,64,256]{2,1,0:T(8,128)(2,1)}, u32[]{:S(2)}) copy-start(bf16[32,64,256]{2,1,0:T(8,128)(2,1)} %final.1) | copy-start | bytes 3145732
  4.9 0.9 %copy-start.2 = (f32[2,64,256]{2,1,0:T(8,128)S(1)}, f32[2,64,256]{2,1,0:T(8,128)}, u32[]{:S(2)}) copy-start(f32[2,64,256]{2,1,0:T(8,128)} %prey.1) | copy-start | bytes 393220
  5.8 0.9 %copy-start.3 = (f32[2,64,256]{2,1,0:T(8,128)S(1)}, f32[2,64,256]{2,1,0:T(8,128)}, u32[]{:S(2)}) copy-start(f32[2,64,256]{2,1,0:T(8,128)} %heat.1) | copy-start | bytes 393220
  6.8 0.8 %copy-start.4 = (s32[64,256]{1,0:T(8,128)S(1)}, s32[64,256]{1,0:T(8,128)}, u32[]{:S(2)}) copy-start(s32[64,256]{1,0:T(8,128)} %sea_in.1) | copy-start | bytes 196612
  7.6 0.8 %copy-start.5 = (f32[64,256]{1,0:T(8,128)S(1)}, f32[64,256]{1,0:T(8,128)}, u32[]{:S(2)}) copy-start(f32[64,256]{1,0:T(8,128)} %fish.1) | copy-start | bytes 196612
  8.4 0.8 %copy-start.6 = (f32[64,256]{1,0:T(8,128)S(1)}, f32[64,256]{1,0:T(8,128)}, u32[]{:S(2)}) copy-start(f32[64,256]{1,0:T(8,128)} %offspring.1) | copy-start | bytes 196612
  9.3 0.8 %copy-start.7 = (f32[32,2,32]{2,1,0:T(2,128)S(1)}, f32[32,2,32]{2,1,0:T(2,128)}, u32[]{:S(2)}) copy-start(f32[32,2,32]{2,1,0:T(2,128)} %landing.1) | copy-start | bytes 24580
  10.0 0.7 %copy-start.8 = (f32[32]{0:T(128)S(1)}, f32[32]{0:T(128)}, u32[]{:S(2)}) copy-start(f32[32]{0:T(128)} %gear.1) | copy-start | bytes 388
  10.7 0.7 %copy-start.9 = (f32[32]{0:T(128)S(1)}, f32[32]{0:T(128)}, u32[]{:S(2)}) copy-start(f32[32]{0:T(128)} %spread.1) | copy-start | bytes 388
  11.3 0.7 %copy-start.10 = (f32[32]{0:T(128)S(1)}, f32[32]{0:T(128)}, u32[]{:S(2)}) copy-start(f32[32]{0:T(128)} %drift.1) | copy-start | bytes 388
  12.0 0.7 %copy-start.11 = (f32[32]{0:T(128)S(1)}, f32[32]{0:T(128)}, u32[]{:S(2)}) copy-start(f32[32]{0:T(128)} %level.1) | copy-start | bytes 388
  12.7 0.7 %copy-start.12 = (f32[32]{0:T(128)S(1)}, f32[32]{0:T(128)}, u32[]{:S(2)}) copy-start(f32[32]{0:T(128)} %death.1) | copy-start | bytes 388
  13.3 0.7 %copy-start.13 = (f32[32]{0:T(128)S(1)}, f32[32]{0:T(128)}, u32[]{:S(2)}) copy-start(f32[32]{0:T(128)} %breed.1) | copy-start | bytes 388
  14.0 0.7 %copy-start.14 = (s32[32]{0:T(128)S(1)}, s32[32]{0:T(128)}, u32[]{:S(2)}) copy-start(s32[32]{0:T(128)} %param.33) | copy-start | bytes 388
  14.6 0.7 %copy-start.15 = (s32[32]{0:T(128)S(1)}, s32[32]{0:T(128)}, u32[]{:S(2)}) copy-start(s32[32]{0:T(128)} %param.34) | copy-start | bytes 388

commit v2 on v1

v2 whole, which is shorter than its diff:
```python
import functools
import itertools
import jax
import jax.numpy as jnp
from jax import lax
from jax.experimental import pallas as pl
from jax.experimental.pallas import tpu as pltpu
from jax.sharding import PartitionSpec as P

LOG2E = 1.4426950408889634
MESH = pl.DeviceIdType.MESH
F32 = jnp.float32
I32 = jnp.int32

AGES = 32
ROWS = 64
LANES = 128
BY = 16
SLOTS = 8
CODE = 64
PAD = 8
FIRST_AGE = 8
FIELD_LANE = 66
GROUP = 8
GIVEN = 20


def iota(shape, dim):
    return lax.broadcasted_iota(I32, shape, dim)


def as_column(row):
    n = row.shape[1]
    eye = iota((n, n), 0) == iota((n, n), 1)
    return jnp.sum(jnp.where(eye, jnp.broadcast_to(row, (n, n)), 0.0), axis=1, keepdims=True)


def as_row(column):
    n = column.shape[0]
    eye = iota((n, n), 0) == iota((n, n), 1)
    return jnp.sum(jnp.where(eye, jnp.broadcast_to(column, (n, n)), 0.0), axis=0, keepdims=True)


def parts(x):
    high = x.astype(jnp.bfloat16)
    left = x - high.astype(F32)
    mid = left.astype(jnp.bfloat16)
    return high, mid, (left - mid.astype(F32)).astype(jnp.bfloat16)


def selected(onehot, x):
    flags = onehot.astype(jnp.bfloat16)
    return sum(jnp.dot(flags, part, preferred_element_type=F32) for part in parts(x))


def repeat(lo, hi, width, fn, carry):
    def step(n, carry):
        for m in range(width):
            carry = fn(lo + n * width + m, carry)
        return carry

    count = (hi - lo) // width
    if count:
        carry = lax.fori_loop(0, count, step, carry)
    for a in range(lo + count * width, hi):
        carry = fn(a, carry)
    return carry


def halves(h):
    return slice(h * LANES, (h + 1) * LANES)


def finished(b, a, rest, fix_col, fix_n, fix_s, blocks, place, recruits, catches, consts):
    rows = slice(b * BY, (b + 1) * BY)
    lane, row = iota((BY, LANES), 1), iota((BY, LANES), 0)
    turned = pltpu.roll(fix_col[rows, :], (LANES - 2 * a) & (LANES - 1), 1)
    made = []
    loss, share, scale = (jnp.broadcast_to(consts[n, pl.ds(a, 1), :], (BY, LANES)) for n in range(3))
    for h in range(2):
        moved = rest[a, h, rows, :] - jnp.where(lane == (0, LANES - 1)[h], turned, 0.0)
        for at, end, fix in ((0, 0, fix_n), (ROWS // BY - 1, BY - 1, fix_s)):
            if b == at:
                edge = jnp.broadcast_to(fix[h, pl.ds(a, 1), :], (BY, LANES))
                moved = moved - jnp.where(row == end, edge, 0.0)
        caught = jnp.broadcast_to(blocks[2 * b + h, pl.ds(place + a, 1), :], (BY, LANES))
        survive = jnp.exp2(loss - share * catches[h])
        made.append(survive * moved + recruits[h] * scale + catches[h] * caught)
    return made


def kernel(sizes, saved, final, *refs):
    given, made, scratch = refs[:GIVEN], refs[GIVEN:GIVEN + 9], refs[GIVEN + 9:]
    local, scratch = scratch[:GIVEN], scratch[GIVEN:]
    (
        prey, heat, sea_in, fish, offspring,
        spread, drift, level, breed,
        gear_v, spread_v, drift_v, level_v, death_v, breed_v,
        landing, east, north, patch, bounds,
    ) = local
    (
        saved_v, final_v, adj1, adj0, rest1, hab, flow,
        forage, warm, sea, open_e, open_s, rec1,
        row_n1, row_s1, row_n0, row_s0,
        halo_n1, halo_s1, halo_n0, halo_s0,
        diag_n1, diag_s1, diag_n0, diag_s0,
        col1, col0, col_w1, col_e1, col_w0, col_e0,
        dcol_w1, dcol_e1, dcol_w0, dcol_e0,
        fix_col1, fix_n1, fix_s1,
        first1, first0, spawn, spawn_a, spawn_s, spawn_b,
        catch_v, catch_out, catch_in, fold_out, fold_in, blocks1,
        local_sem, send_sem, recv_sem,
    ) = scratch
    rest, fix_col, fix_n, fix_s, rec, blocks, consts, fish_out, grad = made
    n_coh, n_lat, n_lon = sizes
    c, i, j = lax.axis_index("coh"), lax.axis_index("lat"), lax.axis_index("lon")
    c_up, c_dn = lax.rem(c + 1, n_coh), lax.rem(c + n_coh - 1, n_coh)
    i_up, i_dn = lax.rem(i + 1, n_lat), lax.rem(i + n_lat - 1, n_lat)
    j_up, j_dn = lax.rem(j + 1, n_lon), lax.rem(j + n_lon - 1, n_lon)
    total_ages = AGES * n_coh

    def at(cc, ii, jj):
        return {"coh": cc, "lat": ii, "lon": jj}

    load_final = pltpu.make_async_copy(final, final_v, local_sem.at[0])
    load_saved = [pltpu.make_async_copy(saved.at[t], saved_v.at[t], local_sem.at[1 + t]) for t in range(2)]
    fetches = [pltpu.make_async_copy(src, dst, local_sem.at[3 + n]) for n, (src, dst) in enumerate(zip(given, local))]
    for copy in fetches[15:] + fetches[:3]:
        copy.start()
    load_final.start()
    for copy in fetches[3:15] + [load_saved[1], load_saved[0]]:
        copy.start()

    barrier = pltpu.get_barrier_semaphore()
    partners = [at(c, i, lax.rem(j + d, n_lon)) for d in range(1, n_lon)]
    partners += [at(c, lax.rem(i + d, n_lat), j) for d in range(1, n_lat)]
    partners += [at(lax.rem(c + d, n_coh), i, j) for d in range(1, n_coh)]
    partners += [at(cc, ii, j) for cc in (c_up, c_dn) for ii in (i_up, i_dn)]
    partners += [at(cc, i, jj) for cc in (c_up, c_dn) for jj in (j_up, j_dn)]
    for partner in partners:
        pl.semaphore_signal(barrier, inc=1, device_id=partner, device_id_type=MESH)

    def remote(src, dst, k, to):
        return pltpu.make_async_remote_copy(
            src_ref=src, dst_ref=dst, send_sem=send_sem.at[k], recv_sem=recv_sem.at[k],
            device_id=to, device_id_type=MESH,
        )

    lane = iota((BY, LANES), 1)
    lane_all = iota((ROWS, LANES), 1)
    even_all = (lane_all & 1) == 0

    def mature(a):
        return (c * AGES + a + 1).astype(F32) * (1.0 / total_ages) * breed[a]

    for copy in fetches[15:]:
        copy.wait()
    east_row = east[...].astype(F32)
    east_col = as_column(east_row)
    same = jnp.broadcast_to(east_col, (32, 32)) == jnp.broadcast_to(east_row, (32, 32))
    ahead = same & (iota((32, 32), 0) < iota((32, 32), 1))
    rank_row = jnp.sum(jnp.where(ahead, 1.0, 0.0), axis=0, keepdims=True)
    slot_row = east_row * SLOTS + rank_row
    code_col = as_column((north[...] * 32 + patch[...]).astype(F32))
    cohort = (c * AGES + iota((32, AGES), 1)).astype(F32)
    lower, upper = (as_column(bounds[n:n + 1, :].astype(F32)) for n in range(2))
    inside = (cohort >= lower) & (cohort < upper)
    catch_v[...] = jnp.broadcast_to(code_col, (32, LANES))
    catch_v[:, 0:32] = jnp.where(inside, landing[:, 0, :], 0.0)
    catch_v[:, 32:64] = jnp.where(inside, landing[:, 1, :], 0.0)
    slots = n_lon * SLOTS
    place = jnp.where(iota((slots, 32), 0).astype(F32) == jnp.broadcast_to(slot_row, (slots, 32)), 1.0, 0.0)
    catch_out[...] = selected(place, catch_v[...]).reshape(n_lon, SLOTS, LANES)
    catch_in[j] = catch_out[j]

    pl.semaphore_wait(barrier, len(partners))

    catch_sends = [
        remote(catch_out.at[lax.rem(j + d, n_lon)], catch_in.at[j], d, at(c, i, lax.rem(j + d, n_lon)))
        for d in range(1, n_lon)
    ]
    for copy in catch_sends:
        copy.start()

    body = slice(0, ROWS)
    for copy in fetches[:3]:
        copy.wait()
    for h in range(2):
        sea[h] = sea_in[:, halves(h)].astype(F32)
    last_lane = lane_all == LANES - 1
    sea0, sea1 = sea[0], sea[1]
    turned1 = pltpu.roll(sea1, LANES - 1, 1)
    open_e[0] = sea0 * jnp.where(last_lane, turned1, pltpu.roll(sea0, LANES - 1, 1))
    open_e[1] = sea1 * jnp.where(last_lane, 0.0, turned1)
    last_row = iota((ROWS, LANES), 0) == ROWS - 1
    pad = jnp.zeros((PAD, LANES), F32)
    for h, here in enumerate((sea0, sea1)):
        open_s[h] = here * jnp.where(last_row, 0.0, pltpu.roll(here, ROWS - 1, 0))
        flow[0, h, 0:PAD, :] = pad
        flow[1, h, 0:PAD, :] = pad
        for t in range(2):
            forage[t, h] = here * prey[t, :, halves(h)]
            warm[t, h] = heat[t, :, halves(h)] * 0.25

    def field(f, h):
        if f == 4:
            return sea[h]
        return (forage, warm)[f % 2][1 - f // 2, h]

    columns = jnp.zeros((ROWS, LANES), F32)
    for h in range(2):
        row_n1[h, 0:8, :] = pad
        row_s1[h, 0:8, :] = pad
    for f in range(5):
        for h in range(2):
            plane = field(f, h)
            row_n1[h, f:f + 1, :] = plane[0:1]
            row_s1[h, f:f + 1, :] = plane[ROWS - 1:ROWS]
        columns = jnp.where(lane_all == FIELD_LANE + 2 * f, jnp.broadcast_to(field(f, 0)[:, 0:1], (ROWS, LANES)), columns)
        columns = jnp.where(
            lane_all == FIELD_LANE + 2 * f + 1, jnp.broadcast_to(field(f, 1)[:, LANES - 1:], (ROWS, LANES)), columns
        )

    def clear_pads(ref, a):
        for h in range(2):
            ref[a, h, ROWS:, :] = pad

    def pick_columns(a, x0, x1):
        width = iota(x0.shape, 1)
        edges = jnp.where(width == 0, x0, x1)
        return ((width + 1) & 127) >> 1 == a, pltpu.roll(edges, 2 * a, 1)

    load_final.wait()

    def unpack(a, columns):
        x = final_v[a].astype(F32)
        x0, x1 = x[:, :LANES], x[:, LANES:]
        clear_pads(adj1, a)
        clear_pads(adj0, a)
        for h, xh in enumerate((x0, x1)):
            adj1[a, h, body, :] = xh
            row_n1[h, pl.ds(FIRST_AGE + a, 1), :] = xh[0:1]
            row_s1[h, pl.ds(FIRST_AGE + a, 1), :] = xh[ROWS - 1:]
        mine, moved = pick_columns(a, x0, x1)
        return jnp.where(mine, moved, columns)

    col1[...] = repeat(0, AGES, 8, unpack, columns)
    clear_pads(adj1, AGES)
    clear_pads(adj0, AGES)

    k_fold, k_spawn, k_month = 16, 20, 28

    def month_copies(t):
        k = k_month + 12 * (1 - t)
        adj = (adj0, adj1)[t]
        col = (col0, col1)[t]
        span = slice(0, 40) if t == 1 else slice(FIRST_AGE, 40)
        row_n, row_s = ((row_n0, row_s0), (row_n1, row_s1))[t]
        halo_n, halo_s = ((halo_n0, halo_s0), (halo_n1, halo_s1))[t]
        diag_n, diag_s = ((diag_n0, diag_s0), (diag_n1, diag_s1))[t]
        col_w, col_e = ((col_w0, col_e0), (col_w1, col_e1))[t]
        dcol_w, dcol_e = ((dcol_w0, dcol_e0), (dcol_w1, dcol_e1))[t]
        first = (first0, first1)[t]
        side = [
            remote(row_n.at[:, span, :], halo_s.at[:, span, :], k, at(c, i_dn, j)),
            remote(row_s.at[:, span, :], halo_n.at[:, span, :], k + 1, at(c, i_up, j)),
            remote(col, col_e, k + 4, at(c, i, j_dn)),
            remote(col, col_w, k + 5, at(c, i, j_up)),
        ]
        younger = [
            remote(adj.at[0, :, body, :], adj.at[AGES, :, body, :], k + 8, at(c_dn, i, j)),
            remote(adj.at[0, :, 0:8, :], diag_s, k + 2, at(c_dn, i_dn, j)),
            remote(adj.at[0, :, ROWS - 8:ROWS, :], diag_n, k + 3, at(c_dn, i_up, j)),
            remote(col, dcol_e, k + 6, at(c_dn, i, j_dn)),
            remote(col, dcol_w, k + 7, at(c_dn, i, j_up)),
        ]
        root = [remote(adj.at[0, :, body, :], first, k + 8 + d, at(d, i, j)) for d in range(1, n_coh)]
        return side, younger, root

    def start_planes(t):
        side, younger, root = month_copies(t)
        adj, first = (adj0, adj1)[t], (first0, first1)[t]

        @pl.when(c > 0)
        def _():
            for copy in younger[:3]:
                copy.start()

        @pl.when(c == 0)
        def _():
            for copy in root:
                copy.start()
            for h in range(2):
                first[h] = adj[0, h, body, :]

    def start_edges(t):
        side, younger, root = month_copies(t)
        for copy in side:
            copy.start()

        @pl.when(c > 0)
        def _():
            for copy in younger[3:]:
                copy.start()

    start_planes(1)
    start_edges(1)

    pair = (c + 1 - 2 * lax.rem(c, 2), n_coh - 1 - c)

    def spawn_copies(t):
        one = [remote(spawn.at[t, h], spawn_a.at[t, h], k_spawn + 2 * t + h, at(pair[h], i, j)) for h in range(2)]
        two = [
            remote(spawn_s.at[t, h], spawn_b.at[t, h], k_spawn + 4 + 2 * t + h, at(pair[1 - h], i, j)) for h in range(2)
        ]
        return one, two

    def spawn_part(t):
        def add(a, total):
            return total + mature(a) * saved_v[t, a].astype(F32)

        load_saved[t].wait()
        total = repeat(0, AGES, 8, add, jnp.zeros((ROWS, 2 * LANES), F32))
        for h in range(2):
            spawn[t, h] = total[:, halves(h)]
        for copy in spawn_copies(t)[0]:
            copy.start()

    def spawn_turn(t):
        one, two = spawn_copies(t)
        for h in range(2):
            one[h].wait_recv()
            spawn_s[t, h] = spawn[t, h] + spawn_a[t, h]
            two[h].start()

    for copy in fetches[3:15]:
        copy.wait()
    spawn_part(1)
    spawn_part(0)
    fish_out[...] = fish[...]
    seniority = (c * AGES + iota((AGES, LANES), 0) + 1).astype(F32) * (1.0 / total_ages)
    consts[0] = jnp.broadcast_to(as_column(death_v[...]) * -LOG2E, (AGES, LANES))
    consts[1] = jnp.broadcast_to(as_column(gear_v[...]) * LOG2E, (AGES, LANES))
    consts[2] = jnp.broadcast_to(as_column(breed_v[...]), (AGES, LANES)) * seniority

    def habitats(t):
        def step(a, carry):
            drift_a, level_a = drift[a], level[a] * 0.25
            for h in range(2):
                for r in range(0, ROWS, BY):
                    rows = slice(r, r + BY)
                    q = warm[t, h, rows, :] - level_a
                    hab[a, h, rows, :] = forage[t, h, rows, :] * drift_a / (1.0 + q * q)
            if t == 1:
                clear_pads(hab, a)
            return carry

        repeat(0, AGES, 4, step, 0)

    def interior(adj, into, a, flow):
        spread_a = spread[a]
        turn = LANES - 1
        for r in range(0, ROWS, BY):
            mid, dn = slice(r, r + BY), slice(r + 1, r + 1 + BY)
            h0, h1 = hab[a, 0, mid, :], hab[a, 1, mid, :]
            l0, l1 = adj[a + 1, 0, mid, :], adj[a + 1, 1, mid, :]
            hr1, lr1 = pltpu.roll(h1, turn, 1), pltpu.roll(l1, turn, 1)
            hr0 = jnp.where(lane == turn, hr1, pltpu.roll(h0, turn, 1))
            lr0 = jnp.where(lane == turn, lr1, pltpu.roll(l0, turn, 1))
            kept, given = [], []
            for h, hh, ll, hr, lr in ((0, h0, l0, hr0, lr0), (1, h1, l1, hr1, lr1)):
                g = hr - hh
                k = jnp.maximum(g, 0.0) + spread_a
                o = open_e[h, mid, :] * (ll - lr)
                y = ll - k * o
                given.append((k - g) * o)
                g = hab[a, h, dn, :] - hh
                k = jnp.maximum(g, 0.0) + spread_a
                o = open_s[h, mid, :] * (ll - adj[a + 1, h, dn, :])
                flow[h, dn, :] = (k - g) * o
                kept.append(y - k * o)
            m0, m1 = pltpu.roll(given[0], 1, 1), pltpu.roll(given[1], 1, 1)
            into[a, 0, mid, :] = kept[0] + (flow[0, mid, :] + jnp.where(lane == 0, m1, m0))
            into[a, 1, mid, :] = kept[1] + (flow[1, mid, :] + jnp.where(lane == 0, m0, m1))

    def interiors(t, lo, hi):
        adj, into = (adj0, adj1)[t], (rest, rest1)[t]
        turns = itertools.count()

        def step(a, carry):
            interior(adj, into, a, flow.at[next(turns) % 2])
            return carry

        repeat(lo, hi, 2, step, 0)

    age_of = iota((AGES, LANES), 0)
    lane_age = ((iota((AGES, LANES), 1) + 1) & 127) >> 1

    def by_row(v):
        return as_column(v[...])

    def by_lane(v):
        wide = jnp.broadcast_to(by_row(v), (AGES, LANES))
        return jnp.sum(jnp.where(age_of == lane_age, wide, 0.0), axis=0, keepdims=True)

    north_open = jnp.where(i > 0, 1.0, 0.0)
    south_open = jnp.where(i < n_lat - 1, 1.0, 0.0)
    west_open = jnp.where(j > 0, 1.0, 0.0)
    east_open = jnp.where(j < n_lon - 1, 1.0, 0.0)

    def edges(t):
        adj = (adj0, adj1)[t]
        side, younger, root = month_copies(t)
        halo_n, halo_s = ((halo_n0, halo_s0), (halo_n1, halo_s1))[t]
        row_n, row_s = ((row_n0, row_s0), (row_n1, row_s1))[t]
        diag_n, diag_s = ((diag_n0, diag_s0), (diag_n1, diag_s1))[t]
        col = (col0, col1)[t]
        col_w, col_e = ((col_w0, col_e0), (col_w1, col_e1))[t]
        dcol_w, dcol_e = ((dcol_w0, dcol_e0), (dcol_w1, dcol_e1))[t]
        for copy in side:
            copy.wait_recv()

        @pl.when(c < n_coh - 1)
        def _():
            for copy in younger[1:]:
                copy.wait_recv()

        @pl.when(c == n_coh - 1)
        def _():
            diag_n[...] = jnp.zeros_like(diag_n)
            diag_s[...] = jnp.zeros_like(diag_s)
            dcol_w[...] = jnp.zeros_like(dcol_w)
            dcol_e[...] = jnp.zeros_like(dcol_e)

        past = FIRST_AGE + AGES
        for h in range(2):
            row_n[h, past:past + 1, :] = adj[AGES, h, 0:1, :]
            row_s[h, past:past + 1, :] = adj[AGES, h, ROWS - 1:ROWS, :]
            halo_n[h, past:past + 1, :] = diag_n[h, 7:8, :]
            halo_s[h, past:past + 1, :] = diag_s[h, 0:1, :]
        later = slice(FIRST_AGE + 1, FIRST_AGE + 1 + AGES)
        f = 2 * (1 - t)
        to_col, to_n, to_s = ((fix_col, fix_n, fix_s), (fix_col1, fix_n1, fix_s1))[t]
        spread_r, drift_r, level_r = (
            jnp.broadcast_to(x, (AGES, LANES)) for x in (by_row(spread_v), by_row(drift_v), by_row(level_v) * 0.25)
        )
        for own, halo, own1, halo1, gate, fix in (
            (row_n, halo_n, row_n1, halo_n1, north_open, to_n),
            (row_s, halo_s, row_s1, halo_s1, south_open, to_s),
        ):
            for h in range(2):
                def habitat(buf):
                    q = buf[h, f + 1:f + 2, :] - level_r
                    return buf[h, f:f + 1, :] * drift_r / (1.0 + q * q)

                passage = own1[h, 4:5, :] * halo1[h, 4:5, :] * gate
                k = spread_r + jnp.maximum(habitat(halo1) - habitat(own1), 0.0)
                fix[h] = passage * k * (own[h, later, :] - halo[h, later, :])

        def both(own_w, own_e):
            wide = (ROWS, LANES)
            return jnp.where(even_all, jnp.broadcast_to(own_w, wide), jnp.broadcast_to(own_e, wide))

        def own_field(f):
            return both(field(f, 0)[:, 0:1], field(f, 1)[:, LANES - 1:])

        def halo_field(f):
            spot = FIELD_LANE + 2 * f
            return both(col_w1[:, spot + 1:spot + 2], col_e1[:, spot:spot + 1])

        spread_l, drift_l, level_l = (by_lane(x) for x in (spread_v, drift_v, level_v))

        def habitat_columns(get):
            q = get(f + 1) - level_l * 0.25
            return get(f) * drift_l / (1.0 + q * q)

        passage = own_field(4) * halo_field(4) * jnp.where(even_all, west_open, east_open)
        mine, moved = pick_columns(AGES, adj[AGES, 0, body, :], adj[AGES, 1, body, :])
        own = pltpu.roll(jnp.where(mine, moved, col[...]), LANES - 2, 1)
        other = jnp.where(even_all, pltpu.roll(col_w[...], LANES - 1, 1), pltpu.roll(col_e[...], LANES - 3, 1))
        other = jnp.where(lane_all == 62, pltpu.roll(dcol_w[...], 63, 1), other)
        other = jnp.where(lane_all == 61, pltpu.roll(dcol_e[...], 61, 1), other)
        k = spread_l + jnp.maximum(habitat_columns(halo_field) - habitat_columns(own_field), 0.0)
        to_col[...] = passage * k * (own - other)

    def finish_one():
        def put(b, a, columns, recruits, catches):
            made = finished(b, a, rest1, fix_col1, fix_n1, fix_s1, blocks1, 0, recruits, catches, consts)
            for h in range(2):
                adj0[a, h, b * BY:(b + 1) * BY, :] = made[h]
                if b == 0:
                    row_n0[h, pl.ds(FIRST_AGE + a, 1), :] = made[h][0:1]
                if b == ROWS // BY - 1:
                    row_s0[h, pl.ds(FIRST_AGE + a, 1), :] = made[h][BY - 1:]
            mine, moved = pick_columns(a, made[0], made[1])
            return jnp.where(mine, moved, columns)

        def block(b):
            rows = slice(b * BY, (b + 1) * BY)
            return rows, [rec1[h, rows, :] for h in range(2)], [fish[rows, halves(h)] for h in range(2)]

        for b in range(ROWS // BY):
            rows, recruits, catches = block(b)
            col0[rows, :] = put(b, 0, jnp.zeros((BY, LANES), F32), recruits, catches)
        start_planes(0)
        for b in range(ROWS // BY):
            rows, recruits, catches = block(b)

            def step(group, columns):
                for n in range(GROUP):
                    columns = put(b, group * GROUP + n, columns, recruits, catches)
                return columns

            columns = col0[rows, :]
            for a in range(1, GROUP):
                columns = put(b, a, columns, recruits, catches)
            col0[rows, :] = lax.fori_loop(1, AGES // GROUP, step, columns)
        start_edges(0)

    def last_cohort(t):
        adj = (adj0, adj1)[t]
        side, younger, root = month_copies(t)

        @pl.when(c < n_coh - 1)
        def _():
            younger[0].wait_recv()

        @pl.when(c == n_coh - 1)
        def _():
            for h in range(2):
                adj[AGES, h, body, :] = jnp.zeros((ROWS, LANES), F32)

        interiors(t, AGES - 1, AGES)

    def recruit(t):
        first = (first0, first1)[t]
        side, younger, root = month_copies(t)
        for d in range(1, n_coh):
            @pl.when(c == d)
            def _():
                root[d - 1].wait_recv()
        two = spawn_copies(t)[1]
        for h in range(2):
            two[h].wait_recv()
            total = spawn_s[t, h] + spawn_b[t, h]
            ratio = 1.0 / (1.0 + total)
            base = first[h] * sea[h]
            (rec, rec1)[t][h] = base * offspring[:, halves(h)] * ratio * ratio
            gain = base * total * ratio
            if t == 1:
                grad[:, halves(h)] = gain
            else:
                grad[:, halves(h)] = grad[:, halves(h)] + gain

    fold_sends = [
        remote(fold_out.at[lax.rem(i + d, n_lat)], fold_in.at[i], k_fold + d, at(c, lax.rem(i + d, n_lat), j))
        for d in range(1, n_lat)
    ]

    habitats(1)
    interiors(1, 0, 14)
    for copy in catch_sends:
        copy.wait_recv()
    got = catch_in[...].reshape(slots, LANES)
    codes = n_lat * 32
    code_row = as_row(got[:, CODE:CODE + 1])
    pick = jnp.where(iota((codes, slots), 0).astype(F32) == jnp.broadcast_to(code_row, (codes, slots)), 1.0, 0.0)
    fold_out[...] = selected(pick, got).reshape(n_lat, 32, LANES)
    fold_in[i] = fold_out[i]
    for copy in fold_sends:
        copy.start()
    spawn_turn(1)
    spawn_turn(0)
    interiors(1, 14, AGES - 1)
    last_cohort(1)
    habitats(0)
    edges(1)
    recruit(1)
    for copy in fold_sends:
        copy.wait_recv()
    block = fold_in[0]
    for d in range(1, n_lat):
        block = block + fold_in[d]
    cells = 2 * LANES * (ROWS // BY)

    def spread_blocks(t, to):
        stack = jnp.concatenate(
            [part.astype(F32) for part in parts(block[:, t * AGES:(t + 1) * AGES])], axis=0
        ).astype(jnp.bfloat16)
        widen = jnp.where((iota((96, cells), 0) & 31) == iota((96, cells), 1) >> 5, 1.0, 0.0).astype(jnp.bfloat16)
        planes = lax.dot_general(stack, widen, (((0,), (0,)), ((), ())), preferred_element_type=F32)
        gear_r = jnp.broadcast_to(by_row(gear_v), (AGES, LANES))
        for b in range(cells // LANES):
            to[b] = planes[:, b * LANES:(b + 1) * LANES] * gear_r

    spread_blocks(1, blocks1)
    finish_one()

    spread_blocks(0, blocks)
    interiors(0, 0, AGES - 1)
    last_cohort(0)
    edges(0)
    recruit(0)

    for copy in catch_sends + fold_sends:
        copy.wait_send()
    for t in range(2):
        side, younger, root = month_copies(t)
        one, two = spawn_copies(t)
        for copy in side + one + two:
            copy.wait_send()

        @pl.when(c > 0)
        def _():
            for copy in younger:
                copy.wait_send()

        @pl.when(c == 0)
        def _():
            for copy in root:
                copy.wait_send()

def combine(rest, fix_col, fix_n, fix_s, rec, blocks, consts, fish, grad, out, grad_out, out_v, out_sem):
    ends = [pltpu.make_async_copy(grad, grad_out, out_sem.at[ROWS // BY])]
    ends[0].start()
    for b in range(ROWS // BY):
        rows = slice(b * BY, (b + 1) * BY)
        recruits = [rec[h, rows, :] for h in range(2)]
        catches = [fish[rows, halves(h)] for h in range(2)]

        def step(a, carry):
            made = finished(b, a, rest, fix_col, fix_n, fix_s, blocks, 0, recruits, catches, consts)
            for h in range(2):
                out_v[a, rows, halves(h)] = made[h]
            return carry

        repeat(0, AGES, GROUP, step, 0)
        span = pl.ds(b * BY, BY)
        ends.append(pltpu.make_async_copy(out_v.at[:, span, :], out.at[:, span, :], out_sem.at[b]))
        ends[-1].start()
    for copy in ends:
        copy.wait()


def shards(
    sizes,
    saved, final, prey, heat, sea, fish, offspring,
    death, gear, spread, drift, level, breed,
    landing, east, north, patch, bounds,
):
    n_coh, n_lat, n_lon = sizes
    hbm = pl.BlockSpec(memory_space=pltpu.HBM)
    vmem = pl.BlockSpec(memory_space=pltpu.VMEM)
    given = [
        prey, heat, sea, fish, offspring, spread, drift, level, breed,
        *[v.reshape(1, -1) for v in (gear, spread, drift, level, death, breed)],
        landing, *[v.reshape(1, -1) for v in (east, north, patch)], bounds.T,
    ]
    spaces = [pltpu.VMEM] * 5 + [pltpu.SMEM] * 4 + [pltpu.VMEM] * 11
    plane = (2, ROWS, LANES)
    padded = (AGES + 1, 2, ROWS + PAD, LANES)
    edge_rows, tile, column = (2, 48, LANES), (2, 8, LANES), (ROWS, LANES)
    made = [
        (AGES, *plane), column, (2, AGES, LANES), (2, AGES, LANES), plane,
        (2 * ROWS // BY, AGES, LANES), (3, AGES, LANES), (ROWS, 2 * LANES), (ROWS, 2 * LANES),
    ]

    def f32(shape):
        return pltpu.VMEM(shape, F32)

    scratch = [space(v.shape, v.dtype) for space, v in zip(spaces, given)] + [
        pltpu.VMEM((2, AGES, ROWS, 2 * LANES), jnp.bfloat16),
        pltpu.VMEM((AGES, ROWS, 2 * LANES), jnp.bfloat16),
        f32(padded), f32(padded), f32(made[0]), f32(padded), f32((2, 2, ROWS + PAD, LANES)),
        f32((2, *plane)), f32((2, *plane)), f32(plane), f32(plane), f32(plane), f32(plane),
        *[f32(edge_rows) for _ in range(8)],
        *[f32(tile) for _ in range(4)],
        *[f32(column) for _ in range(10)],
        f32(column), f32(made[2]), f32(made[3]),
        f32(plane), f32(plane), *[f32((2, *plane)) for _ in range(4)],
        f32((32, LANES)), f32((n_lon, SLOTS, LANES)), f32((n_lon, SLOTS, LANES)),
        f32((n_lat, 32, LANES)), f32((n_lat, 32, LANES)),
        f32(made[5]),
        pltpu.SemaphoreType.DMA((3 + GIVEN,)),
        pltpu.SemaphoreType.DMA((52,)),
        pltpu.SemaphoreType.DMA((52,)),
    ]
    states = pl.pallas_call(
        functools.partial(kernel, sizes),
        out_shape=[jax.ShapeDtypeStruct(shape, F32) for shape in made],
        in_specs=[hbm] * (2 + GIVEN),
        out_specs=[vmem] * len(made),
        scratch_shapes=scratch,
        compiler_params=pltpu.CompilerParams(
            collective_id=0, has_side_effects=True, vmem_limit_bytes=32 * 1024 * 1024
        ),
    )(*[pltpu.with_memory_space_constraint(v, pltpu.HBM) for v in (saved, final, *given)])
    return pl.pallas_call(
        combine,
        out_shape=(
            jax.ShapeDtypeStruct((AGES, ROWS, 2 * LANES), F32),
            jax.ShapeDtypeStruct((ROWS, 2 * LANES), F32),
        ),
        in_specs=[vmem] * len(made),
        out_specs=(hbm, hbm),
        scratch_shapes=[f32((AGES, ROWS, 2 * LANES)), pltpu.SemaphoreType.DMA((ROWS // BY + 1,))],
        compiler_params=pltpu.CompilerParams(vmem_limit_bytes=8 * 1024 * 1024),
    )(*states)


def solution(mesh):
    sizes = tuple(mesh.shape[axis] for axis in ("coh", "lat", "lon"))
    tile = P("lat", "lon")
    months = P(None, "lat", "lon")
    rows = ("lat", "lon")
    in_specs = (
        P(None, "coh", "lat", "lon"), P("coh", "lat", "lon"), months, months, tile, tile, tile,
        *[P("coh")] * 6,
        P(rows, None, "coh"), P(rows, None), P(rows), P(rows), P(rows, None),
    )
    out_specs = (P("coh", "lat", "lon"), tile)
    return jax.shard_map(
        functools.partial(shards, sizes), mesh=mesh, in_specs=in_specs, out_specs=out_specs, check_vma=False
    )
```

time: 53.8 us -> 31.4 us (0.58)
  local copies, waits for them, and re-layouts: 16.6 us -> 0 us
  Pallas kernels: 36.1 us -> 30.7 us
    unnamed x36 -> x0, local copies, waits for them, and re-layouts: 16.6 us -> none
    pallas_call x1 -> x2, Pallas kernels: 36.1 us -> 30.7 us  [the longest x1 28.3 us: shards(): pl.pallas_call(functools.partial(kernel, sizes), out_shape=[jax.ShapeDtyp...]
where the time goes in v2:
time: 31.4 us; the launch traced here: 31.3 us
  Pallas kernels  30.7 us (98%)
  between operations  0.65 us (2%)
    pallas_call x1, Pallas kernels, shards(): pl.pallas_call(functools.partial(kernel, sizes), out_shape=[jax.ShapeDtyp...  28.3 us
    pallas_call x1, Pallas kernels, shards(): pl.pallas_call(combine, out_shape=(jax.ShapeDtypeStruct((AGES, ROWS, 2 *...  2.39 us

profile of v2, /device:TPU:1, one launch (start us, length us, event | category | flops | bytes accessed | tf_op | source)
XLA Modules:
  0.0 31.3 jit_solution(12660034185927843611)
XLA Ops:
  0.6 28.3 %shard_map.185 = (f32[32,2,64,128]{3,2,1,0:T(8,128)S(1)}, f32[64,128]{1,0:T(8,128)S(1)}, f32[2,32,128]{2,1,0:T(8,128)S(1)}, f32[2,32,128]{2,1,0:T(8,128)S(1)}, f...) custom-call(bf16[2,32,64,256]{3,2,1,0:T(8,128)(2,1)} %saved.1, ...), custom_call_target="tpu_custom_call" | custom-call | tf_op jit(solution)/shard_map/pallas_call | solution.py:688
  28.9 2.4 %shard_map.186 = (f32[32,64,256]{2,1,0:T(8,128)}, f32[64,256]{1,0:T(8,128)}) custom-call(f32[32,2,64,128]{3,2,1,0:T(8,128)S(1)} %get-tuple-element.11.rest, f32[64,128]{1,0:T(8,128)S(1)} %get-tuple-element.12.fix_col, f32[2,32,128]{2,1,0:T(8,128)S(1)} %get-tuple-element.13.fix_n, f32[2,32,128]{2,1,0:T(8,128)S(1)} %get-tuple-element.14.fix_s, ...), custom_call_target="tpu_custom_call" | custom-call | tf_op jit(solution)/shard_map/pallas_call | solution.py:698

commit v3 on v2

--- a/solution.py
+++ b/solution.py
@@ -16,7 +16,7 @@
 ROWS = 64
 LANES = 128
 BY = 16
-SLOTS = 8
+SLOTS = 4
 CODE = 64
 PAD = 8
 FIRST_AGE = 8
@@ -74,7 +74,7 @@
 def finished(b, a, rest, fix_col, fix_n, fix_s, blocks, place, recruits, catches, consts):
     rows = slice(b * BY, (b + 1) * BY)
     lane, row = iota((BY, LANES), 1), iota((BY, LANES), 0)
-    turned = pltpu.roll(fix_col[rows, :], (LANES - 2 * a) & (LANES - 1), 1)
+    turned = fix_col[a, rows, :]
     made = []
     loss, share, scale = (jnp.broadcast_to(consts[n, pl.ds(a, 1), :], (BY, LANES)) for n in range(3))
     for h in range(2):
@@ -99,7 +99,7 @@
         landing, east, north, patch, bounds,
     ) = local
     (
-        saved_v, final_v, adj1, adj0, rest1, hab, flow,
+        saved_v, final_v, adj1, adj0, rest1, hab, hab_e, flow,
         forage, warm, sea, open_e, open_s, rec1,
         row_n1, row_s1, row_n0, row_s0,
         halo_n1, halo_s1, halo_n0, halo_s0,
@@ -125,10 +125,8 @@
     load_final = pltpu.make_async_copy(final, final_v, local_sem.at[0])
     load_saved = [pltpu.make_async_copy(saved.at[t], saved_v.at[t], local_sem.at[1 + t]) for t in range(2)]
     fetches = [pltpu.make_async_copy(src, dst, local_sem.at[3 + n]) for n, (src, dst) in enumerate(zip(given, local))]
-    for copy in fetches[15:] + fetches[:3]:
-        copy.start()
-    load_final.start()
-    for copy in fetches[3:15] + [load_saved[1], load_saved[0]]:
+    aged, others = fetches[8], fetches[3:8] + fetches[9:15]
+    for copy in fetches[15:] + [aged, load_saved[1]] + fetches[:3] + [load_final] + others + [load_saved[0]]:
         copy.start()
 
     barrier = pltpu.get_barrier_semaphore()
@@ -182,6 +180,38 @@
     for copy in catch_sends:
         copy.start()
 
+    k_fold, k_spawn, k_month = 16, 20, 28
+
+    pair = (c + 1 - 2 * lax.rem(c, 2), n_coh - 1 - c)
+
+    def spawn_copies(t):
+        one = [remote(spawn.at[t, h], spawn_a.at[t, h], k_spawn + 2 * t + h, at(pair[h], i, j)) for h in range(2)]
+        two = [
+            remote(spawn_s.at[t, h], spawn_b.at[t, h], k_spawn + 4 + 2 * t + h, at(pair[1 - h], i, j)) for h in range(2)
+        ]
+        return one, two
+
+    def spawn_part(t):
+        def add(a, total):
+            return total + mature(a) * saved_v[t, a].astype(F32)
+
+        load_saved[t].wait()
+        total = repeat(0, AGES, 8, add, jnp.zeros((ROWS, 2 * LANES), F32))
+        for h in range(2):
+            spawn[t, h] = total[:, halves(h)]
+        for copy in spawn_copies(t)[0]:
+            copy.start()
+
+    def spawn_turn(t):
+        one, two = spawn_copies(t)
+        for h in range(2):
+            one[h].wait_recv()
+            spawn_s[t, h] = spawn[t, h] + spawn_a[t, h]
+            two[h].start()
+
+    aged.wait()
+    spawn_part(1)
+
     body = slice(0, ROWS)
     for copy in fetches[:3]:
         copy.wait()
@@ -230,6 +260,11 @@
         edges = jnp.where(width == 0, x0, x1)
         return ((width + 1) & 127) >> 1 == a, pltpu.roll(edges, 2 * a, 1)
 
+    def eastward(x0, x1):
+        turned1 = pltpu.roll(x1, LANES - 1, 1)
+        edge = iota(x0.shape, 1) == LANES - 1
+        return jnp.where(edge, turned1, pltpu.roll(x0, LANES - 1, 1)), turned1
+
     load_final.wait()
 
     def unpack(a, columns):
@@ -247,8 +282,6 @@
     col1[...] = repeat(0, AGES, 8, unpack, columns)
     clear_pads(adj1, AGES)
     clear_pads(adj0, AGES)
-
-    k_fold, k_spawn, k_month = 16, 20, 28
 
     def month_copies(t):
         k = k_month + 12 * (1 - t)
@@ -306,36 +339,8 @@
     start_planes(1)
     start_edges(1)
 
-    pair = (c + 1 - 2 * lax.rem(c, 2), n_coh - 1 - c)
-
-    def spawn_copies(t):
-        one = [remote(spawn.at[t, h], spawn_a.at[t, h], k_spawn + 2 * t + h, at(pair[h], i, j)) for h in range(2)]
-        two = [
-            remote(spawn_s.at[t, h], spawn_b.at[t, h], k_spawn + 4 + 2 * t + h, at(pair[1 - h], i, j)) for h in range(2)
-        ]
-        return one, two
-
-    def spawn_part(t):
-        def add(a, total):
-            return total + mature(a) * saved_v[t, a].astype(F32)
-
-        load_saved[t].wait()
-        total = repeat(0, AGES, 8, add, jnp.zeros((ROWS, 2 * LANES), F32))
-        for h in range(2):
-            spawn[t, h] = total[:, halves(h)]
-        for copy in spawn_copies(t)[0]:
-            copy.start()
-
-    def spawn_turn(t):
-        one, two = spawn_copies(t)
-        for h in range(2):
-            one[h].wait_recv()
-            spawn_s[t, h] = spawn[t, h] + spawn_a[t, h]
-            two[h].start()
-
-    for copy in fetches[3:15]:
+    for copy in others:
         copy.wait()
-    spawn_part(1)
     spawn_part(0)
     fish_out[...] = fish[...]
     seniority = (c * AGES + iota((AGES, LANES), 0) + 1).astype(F32) * (1.0 / total_ages)
@@ -346,27 +351,30 @@
     def habitats(t):
         def step(a, carry):
             drift_a, level_a = drift[a], level[a] * 0.25
-            for h in range(2):
-                for r in range(0, ROWS, BY):
-                    rows = slice(r, r + BY)
+            for r in range(0, ROWS, BY):
+                rows = slice(r, r + BY)
+                found = []
+                for h in range(2):
                     q = warm[t, h, rows, :] - level_a
-                    hab[a, h, rows, :] = forage[t, h, rows, :] * drift_a / (1.0 + q * q)
+                    found.append(forage[t, h, rows, :] * drift_a / (1.0 + q * q))
+                    hab[a, h, rows, :] = found[h]
+                if t == 0:
+                    for h, ahead in enumerate(eastward(*found)):
+                        hab_e[a, h, rows, :] = ahead
             if t == 1:
                 clear_pads(hab, a)
             return carry
 
         repeat(0, AGES, 4, step, 0)
 
-    def interior(adj, into, a, flow):
+    def interior(t, adj, into, a, flow):
         spread_a = spread[a]
-        turn = LANES - 1
         for r in range(0, ROWS, BY):
             mid, dn = slice(r, r + BY), slice(r + 1, r + 1 + BY)
             h0, h1 = hab[a, 0, mid, :], hab[a, 1, mid, :]
             l0, l1 = adj[a + 1, 0, mid, :], adj[a + 1, 1, mid, :]
-            hr1, lr1 = pltpu.roll(h1, turn, 1), pltpu.roll(l1, turn, 1)
-            hr0 = jnp.where(lane == turn, hr1, pltpu.roll(h0, turn, 1))
-            lr0 = jnp.where(lane == turn, lr1, pltpu.roll(l0, turn, 1))
+            lr0, lr1 = eastward(l0, l1)
+            hr0, hr1 = eastward(h0, h1) if t == 1 else (hab_e[a, 0, mid, :], hab_e[a, 1, mid, :])
             kept, given = [], []
             for h, hh, ll, hr, lr in ((0, h0, l0, hr0, lr0), (1, h1, l1, hr1, lr1)):
                 g = hr - hh
@@ -388,7 +396,7 @@
         turns = itertools.count()
 
         def step(a, carry):
-            interior(adj, into, a, flow.at[next(turns) % 2])
+            interior(t, adj, into, a, flow.at[next(turns) % 2])
             return carry
 
         repeat(lo, hi, 2, step, 0)
@@ -481,7 +489,9 @@
         other = jnp.where(lane_all == 62, pltpu.roll(dcol_w[...], 63, 1), other)
         other = jnp.where(lane_all == 61, pltpu.roll(dcol_e[...], 61, 1), other)
         k = spread_l + jnp.maximum(habitat_columns(halo_field) - habitat_columns(own_field), 0.0)
-        to_col[...] = passage * k * (own - other)
+        fix = passage * k * (own - other)
+        for a in range(AGES):
+            to_col[a] = pltpu.roll(fix, (LANES - 2 * a) % LANES, 1)
 
     def finish_one():
         def put(b, a, columns, recruits, catches):
@@ -558,29 +568,35 @@
     ]
 
     habitats(1)
+    spawn_turn(1)
     interiors(1, 0, 14)
     for copy in catch_sends:
         copy.wait_recv()
     got = catch_in[...].reshape(slots, LANES)
-    codes = n_lat * 32
+    half = n_lat * 16
     code_row = as_row(got[:, CODE:CODE + 1])
-    pick = jnp.where(iota((codes, slots), 0).astype(F32) == jnp.broadcast_to(code_row, (codes, slots)), 1.0, 0.0)
-    fold_out[...] = selected(pick, got).reshape(n_lat, 32, LANES)
+    wanted = iota((2 * half, slots), 0)
+    low = wanted & (half - 1)
+    code = ((low >> 4) * 32 + (low & 15) + jnp.where(wanted < half, 0, 16)).astype(F32)
+    pick = jnp.where(code == jnp.broadcast_to(code_row, (2 * half, slots)), 1.0, 0.0)
+    folded = selected(pick, got)
+    packed = jnp.where(iota((half, LANES), 1) < 64, folded[:half], pltpu.roll(folded[half:], 64, 1))
+    fold_out[...] = packed.reshape(n_lat, 16, LANES)
     fold_in[i] = fold_out[i]
     for copy in fold_sends:
         copy.start()
-    spawn_turn(1)
-    spawn_turn(0)
     interiors(1, 14, AGES - 1)
     last_cohort(1)
     habitats(0)
     edges(1)
+    spawn_turn(0)
     recruit(1)
     for copy in fold_sends:
         copy.wait_recv()
     block = fold_in[0]
     for d in range(1, n_lat):
         block = block + fold_in[d]
+    block = jnp.concatenate([block, pltpu.roll(block, 64, 1)], axis=0)
     cells = 2 * LANES * (ROWS // BY)
 
     def spread_blocks(t, to):
@@ -596,8 +612,8 @@
     spread_blocks(1, blocks1)
     finish_one()
 
+    interiors(0, 0, AGES - 1)
     spread_blocks(0, blocks)
-    interiors(0, 0, AGES - 1)
     last_cohort(0)
     edges(0)
     recruit(0)
@@ -661,7 +677,7 @@
     padded = (AGES + 1, 2, ROWS + PAD, LANES)
     edge_rows, tile, column = (2, 48, LANES), (2, 8, LANES), (ROWS, LANES)
     made = [
-        (AGES, *plane), column, (2, AGES, LANES), (2, AGES, LANES), plane,
+        (AGES, *plane), (AGES, *column), (2, AGES, LANES), (2, AGES, LANES), plane,
         (2 * ROWS // BY, AGES, LANES), (3, AGES, LANES), (ROWS, 2 * LANES), (ROWS, 2 * LANES),
     ]
 
@@ -671,15 +687,15 @@
     scratch = [space(v.shape, v.dtype) for space, v in zip(spaces, given)] + [
         pltpu.VMEM((2, AGES, ROWS, 2 * LANES), jnp.bfloat16),
         pltpu.VMEM((AGES, ROWS, 2 * LANES), jnp.bfloat16),
-        f32(padded), f32(padded), f32(made[0]), f32(padded), f32((2, 2, ROWS + PAD, LANES)),
+        f32(padded), f32(padded), f32(made[0]), f32(padded), f32(made[0]), f32((2, 2, ROWS + PAD, LANES)),
         f32((2, *plane)), f32((2, *plane)), f32(plane), f32(plane), f32(plane), f32(plane),
         *[f32(edge_rows) for _ in range(8)],
         *[f32(tile) for _ in range(4)],
         *[f32(column) for _ in range(10)],
-        f32(column), f32(made[2]), f32(made[3]),
+        f32(made[1]), f32(made[2]), f32(made[3]),
         f32(plane), f32(plane), *[f32((2, *plane)) for _ in range(4)],
         f32((32, LANES)), f32((n_lon, SLOTS, LANES)), f32((n_lon, SLOTS, LANES)),
-        f32((n_lat, 32, LANES)), f32((n_lat, 32, LANES)),
+        f32((n_lat, 16, LANES)), f32((n_lat, 16, LANES)),
         f32(made[5]),
         pltpu.SemaphoreType.DMA((3 + GIVEN,)),
         pltpu.SemaphoreType.DMA((52,)),

time: 31.4 us -> 30.5 us (0.971)
  Pallas kernels: 30.7 us -> 29.8 us
    pallas_call x1, Pallas kernels: 2.39 us -> 1.73 us  [shards(): pl.pallas_call(combine, out_shape=(jax.ShapeDtypeStruct((AGES, ROWS, 2 *...]
where the time goes in v3:
time: 30.5 us; the launch traced here: 30.4 us
  Pallas kernels  29.8 us (98%)
  between operations  0.65 us (2%)
    pallas_call x1, Pallas kernels, shards(): pl.pallas_call(functools.partial(kernel, sizes), out_shape=[jax.ShapeDtyp...  28 us
    pallas_call x1, Pallas kernels, shards(): pl.pallas_call(combine, out_shape=(jax.ShapeDtypeStruct((AGES, ROWS, 2 *...  1.73 us

profile of v3, /device:TPU:1, one launch (start us, length us, event | category | flops | bytes accessed | tf_op | source)
XLA Modules:
  0.0 30.4 jit_solution(9431350905614694175)
XLA Ops:
  0.6 28.0 %shard_map.185 = (f32[32,2,64,128]{3,2,1,0:T(8,128)S(1)}, f32[32,64,128]{2,1,0:T(8,128)S(1)}, f32[2,32,128]{2,1,0:T(8,128)S(1)}, f32[2,32,128]{2,1,0:T(8,128)S(1...) custom-call(bf16[2,32,64,256]{3,2,1,0:T(8,128)(2,1)} %saved.1, ...), custom_call_target="tpu_custom_call" | custom-call | tf_op jit(solution)/shard_map/pallas_call | solution.py:704
  28.7 1.7 %shard_map.186 = (f32[32,64,256]{2,1,0:T(8,128)}, f32[64,256]{1,0:T(8,128)}) custom-call(f32[32,2,64,128]{3,2,1,0:T(8,128)S(1)} %get-tuple-element.11.rest, f32[32,64,128]{2,1,0:T(8,128)S(1)} %get-tuple-element.12.fix_col, f32[2,32,128]{2,1,0:T(8,128)S(1)} %get-tuple-element.13.fix_n, f32[2,32,128]{2,1,0:T(8,128)S(1)} %get-tuple-element.14.fix_s, ...), custom_call_target="tpu_custom_call" | custom-call | tf_op jit(solution)/shard_map/pallas_call | solution.py:714

commit v4 on v3

--- a/solution.py
+++ b/solution.py
@@ -569,7 +569,7 @@
 
     habitats(1)
     spawn_turn(1)
-    interiors(1, 0, 14)
+    interiors(1, 0, 10)
     for copy in catch_sends:
         copy.wait_recv()
     got = catch_in[...].reshape(slots, LANES)
@@ -585,7 +585,7 @@
     fold_in[i] = fold_out[i]
     for copy in fold_sends:
         copy.start()
-    interiors(1, 14, AGES - 1)
+    interiors(1, 10, AGES - 1)
     last_cohort(1)
     habitats(0)
     edges(1)

time: 30.5 us -> 31 us (1.016)
  Pallas kernels: 29.8 us -> 30.2 us
    pallas_call x1, Pallas kernels: 28 us -> 28.5 us  [shards(): pl.pallas_call(functools.partial(kernel, sizes), out_shape=[jax.ShapeDtyp...]
where the time goes in v4:
time: 31 us; the launch traced here: 30.9 us
  Pallas kernels  30.2 us (97%)
  between operations  0.65 us (2%)
    pallas_call x1, Pallas kernels, shards(): pl.pallas_call(functools.partial(kernel, sizes), out_shape=[jax.ShapeDtyp...  28.5 us
    pallas_call x1, Pallas kernels, shards(): pl.pallas_call(combine, out_shape=(jax.ShapeDtypeStruct((AGES, ROWS, 2 *...  1.73 us

profile of v4, /device:TPU:1, one launch (start us, length us, event | category | flops | bytes accessed | tf_op | source)
XLA Modules:
  0.0 30.9 jit_solution(7705395397181270234)
XLA Ops:
  0.6 28.5 %shard_map.185 = (f32[32,2,64,128]{3,2,1,0:T(8,128)S(1)}, f32[32,64,128]{2,1,0:T(8,128)S(1)}, f32[2,32,128]{2,1,0:T(8,128)S(1)}, f32[2,32,128]{2,1,0:T(8,128)S(1...) custom-call(bf16[2,32,64,256]{3,2,1,0:T(8,128)(2,1)} %saved.1, ...), custom_call_target="tpu_custom_call" | custom-call | tf_op jit(solution)/shard_map/pallas_call | solution.py:704
  29.1 1.7 %shard_map.186 = (f32[32,64,256]{2,1,0:T(8,128)}, f32[64,256]{1,0:T(8,128)}) custom-call(f32[32,2,64,128]{3,2,1,0:T(8,128)S(1)} %get-tuple-element.11.rest, f32[32,64,128]{2,1,0:T(8,128)S(1)} %get-tuple-element.12.fix_col, f32[2,32,128]{2,1,0:T(8,128)S(1)} %get-tuple-element.13.fix_n, f32[2,32,128]{2,1,0:T(8,128)S(1)} %get-tuple-element.14.fix_s, ...), custom_call_target="tpu_custom_call" | custom-call | tf_op jit(solution)/shard_map/pallas_call | solution.py:714
